TPU v7x, 32 devices: a whole 2x2x4 slice. The times are simulated.
32 devices in a mesh: tensor: 4 (over z), example: 8 (over y, x, core).
Axes of the slice: x: 2, y: 2, z: 4, core: 2. Of those that a mesh axis runs over, the one named last changes fastest.
Arguments:
- queries: bfloat16 [1, 4096, 4096], P(None, 'example', 'tensor'), may hold values from -0.0014648438 to 0.0014648438
- basis_out: bfloat16 [4096, 4096], P('example', 'tensor'), may hold values from -0.09375 to 0.09375
- basis_in: bfloat16 [4096, 4096], P('tensor', 'example'), may hold values from -0.09375 to 0.09375
- eigvals: float32 [4096, 4096], P('tensor', 'example'), may hold values from 0.25 to 4
- input_fac: bfloat16 [128, 8, 4096], P('example', None, 'tensor'), may hold values from -6 to 6
- grad_fac: bfloat16 [128, 8, 4096], P('example', None, 'tensor'), may hold values from -6 to 6
- cand_slot: int32 [128], replicated, may hold values from 0 to 127, as said below
- score_list: int32 [8, 16], replicated, may hold values from 0 to 127, as said below
- token_count: int32 [128], replicated, may hold values from 1 to 8
Outputs:
- scores: float32 [1, 128, 8], P(None, 'example')
Inputs may be any that keep to these rules, and one draw needn't show every extreme that they name: `cand_slot`: a permutation; slot s belongs to owner s // 16. `score_list`: every candidate appears exactly once; a scorer's list holds at most 4 candidates of any one owner, and some scorer takes exactly 4 from some owner.
All inputs are finite; a program needn't handle non-finite values.
Results may differ from a plain program's by a relative error of at most 0.019.
Values may be sent and summed in bfloat16 or wider, within the bound.
A program may use at most 128 MiB of HBM per device.

v0:
```python
import jax
import jax.numpy as jnp
from jax import lax
from jax.sharding import PartitionSpec as P


def body(
    queries, basis_out, basis_in, eigvals, input_fac, grad_fac, cand_slot, score_list, token_count
):
    ex_count = lax.axis_size("example")
    my_index = lax.axis_index("example")
    out_rows = lax.all_gather(basis_out, "tensor", axis=1, tiled=True)
    in_rows = lax.all_gather(basis_in, "example", axis=1, tiled=True)
    query_total = queries.shape[0]
    columns = out_rows
    rotated = lax.psum_scatter(
        jnp.einsum("ki,qkj->iqj", columns, queries, preferred_element_type=jnp.float32).astype(
            jnp.bfloat16
        ),
        "example",
        scatter_dimension=0,
        tiled=True,
    )
    columns = in_rows
    core_sum = lax.psum_scatter(
        jnp.einsum("kj,iqk->jqi", columns, rotated, preferred_element_type=jnp.float32).astype(
            jnp.bfloat16
        ),
        "tensor",
        scatter_dimension=0,
        tiled=True,
    ).astype(jnp.float32)
    scaled = (core_sum / eigvals[:, None, :]).astype(jnp.bfloat16)
    columns = out_rows
    turned = jnp.einsum(
        "jqk,ik->jqi",
        lax.all_gather(scaled, "example", axis=2, tiled=True),
        columns,
        preferred_element_type=jnp.float32,
    ).astype(jnp.bfloat16)
    columns = in_rows
    precond = jnp.einsum(
        "jk,kqi->jqi",
        columns,
        lax.all_gather(turned, "tensor", axis=0, tiled=True),
        preferred_element_type=jnp.float32,
    ).astype(jnp.bfloat16)
    cand_total = cand_slot.shape[0]
    cand_dev = input_fac.shape[0]
    token_len = input_fac.shape[1]
    shard_width = input_fac.shape[2]
    list_len = score_list.shape[1]
    cand_ids = jnp.arange(cand_total, dtype=jnp.int32)
    matches = (score_list[:, :, None] == cand_ids[None, None, :]).astype(jnp.int32)
    entry_slot = jnp.sum(matches * cand_slot[None, None, :], axis=2)
    entry_count = jnp.sum(matches * token_count[None, None, :], axis=2)
    entry_owner = entry_slot // cand_dev
    entry_local = entry_slot % cand_dev
    earlier = jnp.arange(list_len)[:, None] > jnp.arange(list_len)[None, :]
    same_owner = entry_owner[:, :, None] == entry_owner[:, None, :]
    entry_rank = jnp.sum((same_owner & earlier[None]).astype(jnp.int32), axis=2)
    capacity = 2 * cand_dev // ex_count
    place_ids = jnp.arange(capacity, dtype=jnp.int32)
    local_ids = jnp.arange(cand_dev, dtype=jnp.int32)
    owned_here = entry_owner == my_index
    send_table = jnp.sum(
        (
            owned_here[:, :, None, None]
            & (entry_rank[:, :, None, None] == place_ids[None, None, :, None])
            & (entry_local[:, :, None, None] == local_ids[None, None, None, :])
        ).astype(jnp.float32),
        axis=1,
    )
    my_owner = lax.dynamic_index_in_dim(entry_owner, my_index, 0, keepdims=False)
    my_rank = lax.dynamic_index_in_dim(entry_rank, my_index, 0, keepdims=False)
    my_count = lax.dynamic_index_in_dim(entry_count, my_index, 0, keepdims=False)
    source_ids = jnp.arange(ex_count, dtype=jnp.int32)
    take_table = (
        (
            (my_owner[:, None, None] == source_ids[None, :, None])
            & (my_rank[:, None, None] == place_ids[None, None, :])
        )
        .astype(jnp.float32)
        .reshape(list_len, ex_count * capacity)
    )
    select_send = send_table.astype(jnp.bfloat16)
    select_take = take_table.astype(jnp.bfloat16)

    def route_rows(owned_rows):
        return jnp.einsum(
            "ers,sx->erx", select_send, owned_rows, preferred_element_type=jnp.float32
        ).astype(jnp.bfloat16)

    def collect_rows(received):
        flat_received = received.reshape(ex_count * capacity, received.shape[2])
        return jnp.dot(select_take, flat_received, preferred_element_type=jnp.float32).astype(
            jnp.bfloat16
        )

    flat_acts = input_fac.reshape(cand_dev, token_len * shard_width)
    flat_grads = grad_fac.reshape(cand_dev, token_len * shard_width)
    sent_acts, sent_grads = (
        lax.all_to_all(route_rows(flat_acts), "example", split_axis=0, concat_axis=0, tiled=True),
        lax.all_to_all(route_rows(flat_grads), "example", split_axis=0, concat_axis=0, tiled=True),
    )
    got_acts = collect_rows(sent_acts).reshape(list_len * token_len, shard_width)
    got_grads = collect_rows(sent_grads).reshape(list_len * token_len, shard_width)
    whole_grads = lax.all_gather(got_grads, "tensor", axis=1, tiled=True)
    columns = whole_grads
    weighted = jnp.einsum(
        "tn,jqn->qtj",
        columns,
        lax.all_gather(precond, "example", axis=2, tiled=True),
        preferred_element_type=jnp.float32,
    )
    partial_scores = jnp.sum(got_acts.astype(jnp.float32)[None] * weighted, axis=2)
    summed = lax.psum(partial_scores, "tensor").reshape(query_total, list_len, token_len)
    live_mask = jnp.arange(token_len, dtype=jnp.int32)[None, :] < my_count[:, None]
    return jnp.where(live_mask[None], summed, jnp.float32(0.0))


def solution(mesh):
    in_specs = (
        P(None, "example", "tensor"),
        P("example", "tensor"),
        P("tensor", "example"),
        P("tensor", "example"),
        P("example", None, "tensor"),
        P("example", None, "tensor"),
        P(),
        P(),
        P(),
    )
    out_specs = P(None, "example", None)
    return jax.shard_map(body, mesh=mesh, in_specs=in_specs, out_specs=out_specs, check_vma=False)
```

profile of v0, /device:TPU:0, one launch (start us, length us, event | category | flops | bytes accessed | tf_op | source)
XLA Modules:
  0.0 568.8 jit_solution(2000959011714621672)
XLA Ops:
  6.5 0.7 all-gather.9.cloned.1.call-update
  7.3 0.7 all-gather.11.cloned.1.call-update
  8.1 84.4 %all-gather.9.cloned.1.call-done = bf16[512,4096]{1,0:T(8,128)(2,1)} async-done(((bf16[512,1024]{1,0:T(8,128)(2,1)}), bf16[512,4096]{1,0:T(8,128)(2,1)}) %all-gather.9.cloned.1.call-update) | async-done | bytes 4194320 | tf_op jit(solution)/shard_map/all_gather | solution.py:12
  92.4 9.0 %convert_bitcast_fusion = bf16[4096,1,1024]{2,0,1:T(8,128)(2,1)} fusion(bf16[512,4096]{1,0:T(8,128)(2,1)} %all-gather.9.cloned.1.call-done, bf16[1,512,1024]{2,1,0:T(8,128)(2,1)S(1)} %copy-done), kind=kOutput, calls=%fused_computation.9 | convolution fusion | flops 4299161600 | bytes 13631488 | tf_op jit(solution)/shard_map/ki,qkj->iqj/dot_general | solution.py:17
  101.5 47.3 %all-gather.11.cloned.1.call-done = bf16[1024,4096]{1,0:T(8,128)(2,1)} async-done(((bf16[1024,512]{1,0:T(8,128)(2,1)}), bf16[1024,4096]{1,0:T(8,128)(2,1)}) %all-gather.11.cloned.1.call-update) | async-done | bytes 8388624 | tf_op jit(solution)/shard_map/all_gather | solution.py:13
  148.8 74.8 %reduce-scatter.3.cloned.1.call-done = bf16[512,1,1024]{2,0,1:T(8,128)(2,1)} async-done(((bf16[4096,1,1024]{2,0,1:T(8,128)(2,1)}), bf16[512,1,1024]{2,0,1:T(8,128)(2,1)}) %reduce-scatter.3.cloned.1.call-update) | async-done | bytes 1048592 | tf_op jit(solution)/shard_map/reduce_scatter | solution.py:16
  223.6 10.2 %fusion.5 = bf16[4096,1,512]{0,2,1:T(8,128)(2,1)} fusion(bf16[1024,4096]{1,0:T(8,128)(2,1)} %all-gather.11.cloned.1.call-done, bf16[512,1,1024]{2,0,1:T(8,128)(2,1)} %reduce-scatter.3.cloned.1.call-done), kind=kOutput, calls=%fused_computation.11 | convolution fusion | flops 4297064448 | bytes 13631488 | tf_op jit(solution)/shard_map/kj,iqk->jqi/dot_general | solution.py:26
  233.9 1.9 copy.26
  235.8 74.9 %reduce-scatter.5.cloned.1.call-done = bf16[1024,1,512]{0,2,1:T(8,128)(2,1)} async-done(((bf16[4096,1,512]{0,2,1:T(8,128)(2,1)}), bf16[1024,1,512]{0,2,1:T(8,128)(2,1)}) %reduce-scatter.5.cloned.1.call-update) | async-done | bytes 1048592 | tf_op jit(solution)/shard_map/reduce_scatter | solution.py:25
  310.7 2.6 fusion.6
  313.6 54.8 %all-gather.13.cloned.1.call-done = bf16[1024,1,4096]{0,2,1:T(8,128)(2,1)} async-done(((bf16[1024,1,512]{0,2,1:T(8,128)(2,1)}), bf16[1024,1,4096]{0,2,1:T(8,128)(2,1)}) %all-gather.13.cloned.1.call-update) | async-done | bytes 8388624 | tf_op jit(solution)/shard_map/all_gather | solution.py:37
  368.4 10.1 %fusion.7 = bf16[1024,512]{1,0:T(8,128)(2,1)} fusion(bf16[512,4096]{1,0:T(8,128)(2,1)} %all-gather.9.cloned.1.call-done, bf16[1024,1,4096]{0,2,1:T(8,128)(2,1)} %all-gather.13.cloned.1.call-done), kind=kOutput, calls=%fused_computation.14 | convolution fusion | flops 4295491584 | bytes 13631488 | tf_op jit(solution)/shard_map/jqk,ik->jqi/dot_general | solution.py:35
  378.7 0.4 select_reduce_fusion.1
  379.1 0.3 convert_reduce_fusion.1
  379.7 0.3 convolution_convert_fusion
  380.0 1.2 copy.28
  381.2 3.5 all-to-all-start.1
  384.8 9.6 %all-to-all-done.1 = bf16[8,4,8192]{2,1,0:T(4,128)(2,1)S(1)} async-done(((bf16[8,4,8192]{2,1,0:T(4,128)(2,1)}), bf16[8,4,8192]{2,1,0:T(4,128)(2,1)S(1)}, u32[]{:S(2)}, u32[]{:S(2)}) %all-to-all-start.1) | async-done | bytes 524320 | tf_op jit(solution)/shard_map/all_to_all | solution.py:104
  394.4 0.4 fusion.2
  394.8 0.9 reshape.265
  396.0 63.5 %all-gather.17.cloned.1.call-done = bf16[4096,512]{1,0:T(8,128)(2,1)} async-done(((bf16[1024,512]{1,0:T(8,128)(2,1)}), bf16[4096,512]{1,0:T(8,128)(2,1)}) %all-gather.17.cloned.1.call-update) | async-done | bytes 4194320 | tf_op jit(solution)/shard_map/all_gather | solution.py:45
  459.4 10.2 %fusion.10 = bf16[1024,512]{0,1:T(8,128)(2,1)} fusion(bf16[4096,512]{1,0:T(8,128)(2,1)} %all-gather.17.cloned.1.call-done, bf16[1024,4096]{1,0:T(8,128)(2,1)} %all-gather.11.cloned.1.call-done), kind=kOutput, calls=%fused_computation.16 | convolution fusion | flops 4295491584 | bytes 13631488 | tf_op jit(solution)/shard_map/jk,kqi->jqi/dot_general | solution.py:42
  469.8 0.3 convolution_convert_fusion.1
  470.1 1.2 copy.24
  471.3 3.7 all-to-all-start
  475.0 9.7 %all-to-all-done = bf16[8,4,8192]{2,1,0:T(4,128)(2,1)S(1)} async-done(((bf16[8,4,8192]{2,1,0:T(4,128)(2,1)}), bf16[8,4,8192]{2,1,0:T(4,128)(2,1)S(1)}, u32[]{:S(2)}, u32[]{:S(2)}) %all-to-all-start) | async-done | bytes 524320 | tf_op jit(solution)/shard_map/all_to_all | solution.py:103
  484.7 0.4 fusion.1
  485.4 2.0 all-gather.15.cloned.1.call-done
  487.5 55.8 %all-gather.19.cloned.1.call-done = bf16[1024,4096]{0,1:T(8,128)(2,1)} async-done(((bf16[1024,512]{0,1:T(8,128)(2,1)}), bf16[1024,4096]{0,1:T(8,128)(2,1)}) %all-gather.19.cloned.1.call-update) | async-done | bytes 8388624 | tf_op jit(solution)/shard_map/all_gather | solution.py:113
  543.3 6.0 %fusion.12 = f32[128]{0:T(128)S(1)} fusion(f32[1,128,1024]{1,2,0:T(8,128)S(1)} %copy.30, bf16[1024,4096]{0,1:T(8,128)(2,1)} %all-gather.19.cloned.1.call-done, bf16[128,4096]{1,0:T(8,128)(2,1)} %all-gather.15.cloned.1.call-done), kind=kOutput, calls=%fused_computation.19 | convolution fusion | flops 1074003840 | bytes 9961984 | tf_op jit(solution)/shard_map/tn,jqn->qtj/dot_general | solution.py:110
  549.4 11.8 %psum.7 = f32[1,16,8]{2,1,0:T(8,128)S(1)} all-reduce(f32[1,16,8]{2,1,0:T(8,128)S(1)} %reshape.266), channel_id=1, replica_groups=mesh['tensor'=4,'example'=8] {'tensor'}, use_global_device_ids=true, to_apply=%region_7.8 | all-reduce | flops 128 | bytes 1024 | tf_op jit(solution)/shard_map/psum | solution.py:117
  561.3 0.7 copy.31
  (42 shorter events, 1.8 us)
Async XLA Ops:
  6.5 85.9 %copy-start = (bf16[1,512,1024]{2,1,0:T(8,128)(2,1)S(1)}, bf16[1,512,1024]{2,1,0:T(8,128)(2,1)}, u32[]{:S(2)}) copy-start(bf16[1,512,1024]{2,1,0:T(8,128)(2,1)} %param.9) | copy-start | bytes 3145732
  6.5 85.9 %all-gather.9.cloned.1.call-start = ((), (), s32[]{:S(2)}) async-start(), calls=%async_computation.4 | async-start | bytes 5242880 | tf_op jit(solution)/shard_map/all_gather | solution.py:12
  7.3 141.6 %all-gather.11.cloned.1.call-start = ((), (), s32[]{:S(2)}) async-start(), calls=%async_computation.6 | async-start | bytes 9437184 | tf_op jit(solution)/shard_map/all_gather | solution.py:13
  8.0 215.6 %reduce-scatter.3.cloned.1.call-start = ((), (), s32[]{:S(2)}) async-start(), calls=%async_computation.5 | async-start | bytes 9437184 | tf_op jit(solution)/shard_map/reduce_scatter | solution.py:16
  101.4 209.3 %reduce-scatter.5.cloned.1.call-start = ((), (), s32[]{:S(2)}) async-start(), calls=%async_computation.7 | async-start | bytes 5242880 | tf_op jit(solution)/shard_map/reduce_scatter | solution.py:25
  233.8 134.6 %all-gather.13.cloned.1.call-start = ((), (), s32[]{:S(2)}) async-start(), calls=%async_computation.8 | async-start | bytes 9437184 | tf_op jit(solution)/shard_map/all_gather | solution.py:37
  313.4 65.1 %copy-start.1 = (bf16[16,8,1024]{2,1,0:T(8,128)(2,1)S(1)}, bf16[16,8,1024]{2,1,0:T(8,128)(2,1)}, u32[]{:S(2)}) copy-start(bf16[16,8,1024]{2,1,0:T(8,128)(2,1)} %param.14) | copy-start | bytes 786436
  313.4 65.3 %copy-start.3 = (s32[8,16]{1,0:T(8,128)S(1)}, s32[8,16]{1,0:T(8,128)}, u32[]{:S(2)}) copy-start(s32[8,16]{1,0:T(8,128)} %param.16) | copy-start | bytes 1540
  313.4 65.3 %copy-start.4 = (s32[128]{0:T(128)S(1)}, s32[128]{0:T(128)}, u32[]{:S(2)}) copy-start(s32[128]{0:T(128)} %param.17) | copy-start | bytes 1540
  313.4 65.3 %copy-start.5 = (s32[128]{0:T(128)S(1)}, s32[128]{0:T(128)}, u32[]{:S(2)}) copy-start(s32[128]{0:T(128)} %param.15) | copy-start | bytes 1540
  313.4 146.0 %all-gather.17.cloned.1.call-start = ((), (), s32[]{:S(2)}) async-start(), calls=%async_computation.10 | async-start | bytes 5242880 | tf_op jit(solution)/shard_map/all_gather | solution.py:45
  381.2 13.2 %all-to-all-start.1 = ((bf16[8,4,8192]{2,1,0:T(4,128)(2,1)}), bf16[8,4,8192]{2,1,0:T(4,128)(2,1)S(1)}, u32[]{:S(2)}, u32[]{:S(2)}) async-start(bf16[8,4,8192]{2,1,0:T(4,128)(2,1)} %copy.28), calls=%async_computation.3 | async-start | bytes 1048576 | tf_op jit(solution)/shard_map/all_to_all | solution.py:104
  384.7 102.8 %all-gather.15.cloned.1.call-start = ((), (), s32[]{:S(2)}) async-start(), calls=%async_computation.9 | async-start | bytes 1310720 | tf_op jit(solution)/shard_map/all_gather | solution.py:108
  395.7 74.0 %copy-start.2 = (bf16[16,8,1024]{2,1,0:T(8,128)(2,1)S(1)}, bf16[16,8,1024]{2,1,0:T(8,128)(2,1)}, u32[]{:S(2)}) copy-start(bf16[16,8,1024]{2,1,0:T(8,128)(2,1)} %param.13) | copy-start | bytes 786436
  395.7 147.6 %all-gather.19.cloned.1.call-start = ((), (), s32[]{:S(2)}) async-start(), calls=%async_computation.11 | async-start | bytes 9437184 | tf_op jit(solution)/shard_map/all_gather | solution.py:113
  471.3 13.4 %all-to-all-start = ((bf16[8,4,8192]{2,1,0:T(4,128)(2,1)}), bf16[8,4,8192]{2,1,0:T(4,128)(2,1)S(1)}, u32[]{:S(2)}, u32[]{:S(2)}) async-start(bf16[8,4,8192]{2,1,0:T(4,128)(2,1)} %copy.24), calls=%async_computation | async-start | bytes 1048576 | tf_op jit(solution)/shard_map/all_to_all | solution.py:103
Sparse Core Ops, SparseCore 0:
  8.9 83.4 all-gather.8
  94.3 54.4 all-gather.10
  152.3 71.2 reduce-scatter.2
  233.9 76.7 reduce-scatter.4
  313.5 54.8 all-gather.12
  378.6 80.7 all-gather.16
  461.0 26.4 all-gather.14
  489.4 53.8 all-gather.18
where the time goes:
time: 569 us
  waiting for transfers between devices  478 us (84%)
  matrix products  46.8 us (8%)
  between operations  13.7 us (2%)
  blocking collectives  11.8 us (2%)
  starting transfers between devices  7.87 us (1%)
  local copies, waits for them, and re-layouts  6.58 us (1%)
    all_gather x1, waiting for transfers between devices, body(): out_rows = lax.all_gather(basis_out, 'tensor', axis=1, tiled=True)  84.4 us
    reduce_scatter x1, waiting for transfers between devices, body(): lax.psum_scatter(jnp.einsum('kj,iqk->jqi', columns, rotated, preferred_el...  74.9 us
    reduce_scatter x1, waiting for transfers between devices, body(): lax.psum_scatter(jnp.einsum('ki,qkj->iqj', columns, queries, preferred_el...  74.8 us
    all_gather x1, waiting for transfers between devices, body(): lax.all_gather(turned, 'tensor', axis=0, tiled=True)  63.5 us
    all_gather x1, waiting for transfers between devices, body(): lax.all_gather(precond, 'example', axis=2, tiled=True)  55.8 us
    all_gather x1, waiting for transfers between devices, body(): lax.all_gather(scaled, 'example', axis=2, tiled=True)  54.8 us
    all_gather x1, waiting for transfers between devices, body(): in_rows = lax.all_gather(basis_in, 'example', axis=1, tiled=True)  47.3 us
    psum x1, blocking collectives, body(): lax.psum(partial_scores, 'tensor').reshape(query_total, list_len, token_len)  11.8 us
  transfers between devices with their start and end apart: 10, of which 10 were waited for; matrix products, arithmetic and copies ran while one was open for 5% of the time, Pallas kernels for 0%

commit v1 on v0

v1 whole, which is shorter than its diff:
```python
import jax
import jax.numpy as jnp
from jax import lax
from jax.sharding import PartitionSpec as P

BF = jnp.bfloat16
F32 = jnp.float32


def regroup_grads(grads, n_tensor, n_example):
    ratio = n_example // n_tensor
    half = grads.shape[1] // ratio
    parity = lax.axis_index("example") % ratio
    received = []
    for shift in range(ratio):
        piece = lax.dynamic_slice_in_dim(grads, ((parity + shift) % ratio) * half, half, 1)
        perm = []
        for t in range(n_tensor):
            for e in range(n_example):
                target = (e // ratio) * n_example + ratio * t + (e + shift) % ratio
                perm.append((t * n_example + e, target))
        received.append(lax.ppermute(piece, ("tensor", "example"), perm))
    stacked = jnp.stack(received)
    order = (parity - jnp.arange(ratio)) % ratio
    pieces = [lax.dynamic_index_in_dim(stacked, order[p], 0, keepdims=False) for p in range(ratio)]
    return jnp.concatenate(pieces, axis=0)


def body(
    queries, basis_out, basis_in, eigvals, input_fac, grad_fac, cand_slot, score_list, token_count
):
    n_example = lax.axis_size("example")
    n_tensor = lax.axis_size("tensor")
    my_index = lax.axis_index("example")
    cand_total = cand_slot.shape[0]
    token_len = input_fac.shape[1]
    list_len = score_list.shape[1]
    query_total, rows, width = queries.shape
    acts = input_fac.reshape(-1, width)
    grads = grad_fac.reshape(-1, width)
    tokens = acts.shape[0]

    in_rows = lax.all_gather(basis_in, "example", axis=1, tiled=True)
    moved_grads = regroup_grads(grads, n_tensor, n_example)
    out_rows = lax.all_gather(basis_out, "tensor", axis=1, tiled=True)
    left = jnp.concatenate([queries.reshape(-1, width), acts], axis=0)
    half_rotated = lax.psum_scatter(
        jnp.einsum("jl,rj->lr", in_rows, left, preferred_element_type=F32).astype(BF),
        "tensor",
        scatter_dimension=0,
        tiled=True,
    )
    split = query_total * rows
    acts_rot = lax.all_gather(half_rotated[:, split:], "example", axis=0)
    parts = [half_rotated[:, q * rows : (q + 1) * rows] for q in range(query_total)]
    right = jnp.concatenate(parts + [moved_grads], axis=0)
    core = lax.psum_scatter(
        jnp.einsum("ik,xi->kx", out_rows, right, preferred_element_type=F32).astype(BF),
        "example",
        scatter_dimension=0,
        tiled=True,
    )
    wide = half_rotated.shape[0]
    grads_rot = lax.all_gather(core[:, query_total * wide :], "tensor", axis=0)
    acts_flat = jnp.transpose(acts_rot, (1, 0, 2)).reshape(wide, -1).astype(F32)
    grads_flat = jnp.transpose(grads_rot, (1, 0, 2)).reshape(core.shape[0], -1)
    partial = []
    for q in range(query_total):
        scaled = (core[:, q * wide : (q + 1) * wide].astype(F32) / eigvals.T).astype(BF)
        weighted = jnp.einsum("kl,kt->lt", scaled, grads_flat, preferred_element_type=F32)
        partial.append(jnp.sum(weighted * acts_flat, axis=0))
    summed = lax.psum(jnp.stack(partial), ("tensor", "example"))
    by_slot = summed.reshape(query_total, cand_total, token_len)

    my_list = lax.dynamic_index_in_dim(score_list, my_index, 0, keepdims=False)
    ids = jnp.arange(cand_total, dtype=jnp.int32)
    matches = my_list[:, None] == ids[None, :]
    my_slot = jnp.sum(jnp.where(matches, cand_slot[None, :], 0), axis=1)
    my_count = jnp.sum(jnp.where(matches, token_count[None, :], 0), axis=1)
    pick = my_slot[:, None] == ids[None, :]
    scores = jnp.sum(jnp.where(pick[None, :, :, None], by_slot[:, None], F32(0.0)), axis=2)
    live = jnp.arange(token_len, dtype=jnp.int32)[None, :] < my_count[:, None]
    return jnp.where(live[None], scores, F32(0.0))


def solution(mesh):
    in_specs = (
        P(None, "example", "tensor"),
        P("example", "tensor"),
        P("tensor", "example"),
        P("tensor", "example"),
        P("example", None, "tensor"),
        P("example", None, "tensor"),
        P(),
        P(),
        P(),
    )
    out_specs = P(None, "example", None)
    return jax.shard_map(body, mesh=mesh, in_specs=in_specs, out_specs=out_specs, check_vma=False)
```

time: 569 us -> 472 us (0.83)
  waiting for transfers between devices: 478 us -> 367 us
  blocking collectives: 11.8 us -> 40.5 us
  matrix products: 46.8 us -> 24.3 us
  local copies, waits for them, and re-layouts: 6.58 us -> 18.4 us
  starting transfers between devices: 7.87 us -> 1.38 us
    all_gather x4 -> x2, waiting for transfers between devices: 176 us -> 43.8 us  [the longest x1 27.7 us: body(): acts_rot = lax.all_gather(half_rotated[:, split:], 'example', axis=0)]
    reduce_scatter x2, waiting for transfers between devices: 150 us -> 181 us  [the longest x1 102 us: body(): lax.psum_scatter(jnp.einsum('jl,rj->lr', in_rows, left, preferred_element...]
    psum x1, blocking collectives: 11.8 us -> 40.5 us  [body(): summed = lax.psum(jnp.stack(partial), ('tensor', 'example'))]
    dot_general x9 -> x3, matrix products: 46.8 us -> 24.3 us  [the longest x1 10.5 us: body(): jnp.einsum('ik,xi->kx', out_rows, right, preferred_element_type=F32)]
    all_to_all x2 -> x0, waiting for transfers between devices: 19.3 us -> none  [the longest x1 9.74 us: body(): lax.all_to_all(route_rows(flat_acts), 'example', split_axis=0, concat_axi...]
    all_gather x1, waiting for transfers between devices: 47.3 us -> 60.6 us  [body(): in_rows = lax.all_gather(basis_in, 'example', axis=1, tiled=True)]
    all_to_all x2 -> x0, starting transfers between devices: 7.19 us -> none  [the longest x1 3.69 us: body(): lax.all_to_all(route_rows(flat_acts), 'example', split_axis=0, concat_axi...]
  transfers between devices with their start and end apart: 10 -> 8, of which waited for: 10 -> 6; matrix products, arithmetic and copies ran while one was open for 5% -> 4% of each run, Pallas kernels for 0% -> 0%
where the time goes in v1:
time: 472 us
  waiting for transfers between devices  367 us (78%)
  blocking collectives  40.5 us (9%)
  matrix products  24.3 us (5%)
  local copies, waits for them, and re-layouts  18.4 us (4%)
  between operations  17.5 us (4%)
    reduce_scatter x1, waiting for transfers between devices, body(): lax.psum_scatter(jnp.einsum('jl,rj->lr', in_rows, left, preferred_element...  102 us
    all_gather x1, waiting for transfers between devices, body(): out_rows = lax.all_gather(basis_out, 'tensor', axis=1, tiled=True)  80.4 us
    reduce_scatter x1, waiting for transfers between devices, body(): lax.psum_scatter(jnp.einsum('ik,xi->kx', out_rows, right, preferred_eleme...  78.3 us
    all_gather x1, waiting for transfers between devices, body(): in_rows = lax.all_gather(basis_in, 'example', axis=1, tiled=True)  60.6 us
    psum x1, blocking collectives, body(): summed = lax.psum(jnp.stack(partial), ('tensor', 'example'))  40.5 us
    all_gather x1, waiting for transfers between devices, body(): acts_rot = lax.all_gather(half_rotated[:, split:], 'example', axis=0)  27.7 us
    all_gather x1, waiting for transfers between devices, body(): grads_rot = lax.all_gather(core[:, query_total * wide:], 'tensor', axis=0)  16.1 us
    dot_general x1, matrix products, body(): jnp.einsum('ik,xi->kx', out_rows, right, preferred_element_type=F32)  10.5 us
  transfers between devices with their start and end apart: 8, of which 6 were waited for; matrix products, arithmetic and copies ran while one was open for 4% of the time, Pallas kernels for 0%

profile of v1, /device:TPU:0, one launch (start us, length us, event | category | flops | bytes accessed | tf_op | source)
XLA Modules:
  0.0 471.9 jit_solution(15291793643969894554)
XLA Ops:
  6.5 0.7 all-gather.7.cloned.1.call-update
  7.3 60.6 %all-gather.7.cloned.1.call-done = bf16[1024,4096]{1,0:T(8,128)(2,1)} async-done(((bf16[1024,512]{1,0:T(8,128)(2,1)}), bf16[1024,4096]{1,0:T(8,128)(2,1)}) %all-gather.7.cloned.1.call-update) | async-done | bytes 8388624 | tf_op jit(solution)/shard_map/all_gather | solution.py:43
  67.9 9.9 %fusion.1 = bf16[4096,640]{0,1:T(8,128)(2,1)} fusion(bf16[1024,4096]{1,0:T(8,128)(2,1)} %all-gather.7.cloned.1.call-done, bf16[128,1024]{1,0:T(8,128)(2,1)} %bitcast.54, bf16[512,1024]{1,0:T(8,128)(2,1)} %bitcast.53), kind=kOutput, calls=%fused_computation.3 | convolution fusion | flops 5373952000 | bytes 14942208 | tf_op jit(solution)/shard_map/jl,rj->lr/dot_general | solution.py:48
  77.9 0.7 all-gather.9.cloned.1.call-update
  78.7 0.1 copy-done.1
  78.8 0.1 copy.23
  78.9 0.7 collective-permute-start
  79.6 0.1 copy.24
  79.7 0.3 collective-permute-start.1
  80.0 0.6 fusion.22
  84.5 0.1 fusion.17
  84.6 102.3 %reduce-scatter.3.cloned.1.call-done = bf16[1024,640]{0,1:T(8,128)(2,1)} async-done(((bf16[4096,640]{0,1:T(8,128)(2,1)}), bf16[1024,640]{0,1:T(8,128)(2,1)}) %reduce-scatter.3.cloned.1.call-update) | async-done | bytes 1310736 | tf_op jit(solution)/shard_map/reduce_scatter | solution.py:47
  186.9 1.3 slice.24
  188.2 80.4 %all-gather.9.cloned.1.call-done = bf16[512,4096]{1,0:T(8,128)(2,1)} async-done(((bf16[512,1024]{1,0:T(8,128)(2,1)}), bf16[512,4096]{1,0:T(8,128)(2,1)}) %all-gather.9.cloned.1.call-update) | async-done | bytes 4194320 | tf_op jit(solution)/shard_map/all_gather | solution.py:45
  268.6 10.5 %fusion = bf16[4096,1280]{0,1:T(8,128)(2,1)} fusion(bf16[512,4096]{1,0:T(8,128)(2,1)} %all-gather.9.cloned.1.call-done, bf16[128,512]{0,1:T(8,128)(2,1)S(1)} %get-tuple-element.8, bf16[128,512]{0,1:T(8,128)(2,1)S(1)} %get-tuple-element.7, bf16[1024,512]{0,1:T(8,128)(2,1)S(1)} %slice.24), kind=kOutput, calls=%fused_computation.1 | convolution fusion | flops 5377884160 | bytes 15990784 | tf_op jit(solution)/shard_map/ik,xi->kx/dot_general | solution.py:58
  279.2 1.7 slice.27
  280.9 0.2 all-gather.11.cloned.1.call-start
  281.2 78.3 %reduce-scatter.5.cloned.1.call-done = bf16[512,1280]{0,1:T(8,128)(2,1)} async-done(((bf16[4096,1280]{0,1:T(8,128)(2,1)}), bf16[512,1280]{0,1:T(8,128)(2,1)}) %reduce-scatter.5.cloned.1.call-update) | async-done | bytes 1310736 | tf_op jit(solution)/shard_map/reduce_scatter | solution.py:57
  359.4 1.7 slice.26
  361.1 0.2 select_reduce_fusion.2
  361.3 0.1 iota_compare_fusion
  361.4 27.7 %all-gather.13.cloned.1.call-done = bf16[8192,128]{0,1:T(8,128)(2,1)} async-done(((bf16[1024,128]{0,1:T(8,128)(2,1)}), bf16[8192,128]{0,1:T(8,128)(2,1)}) %all-gather.13.cloned.1.call-update) | async-done | bytes 2097168 | tf_op jit(solution)/shard_map/all_gather | solution.py:54
  389.1 2.0 convert_element_type.38
  391.1 5.3 %copy.26 = f32[16,8,8,1024]{3,2,1,0:T(8,128)} copy(f32[16,8,8,1024]{3,1,2,0:T(8,128)S(1)} %bitcast.45) | data formatting | bytes 8388608
  396.4 5.9 %copy.20 = f32[1024,8,128]{2,1,0:T(8,128)} copy(f32[1024,8,128]{0,1,2:T(8,128)} %bitcast.46) | data formatting | bytes 8388608 | tf_op jit(solution)/shard_map/convert_element_type | solution.py:65
  402.4 16.1 %all-gather.11.cloned.1.call-done = bf16[2048,256]{0,1:T(8,128)(2,1)} async-done(((bf16[512,256]{0,1:T(8,128)(2,1)}), bf16[2048,256]{0,1:T(8,128)(2,1)}) %all-gather.11.cloned.1.call-update) | async-done | bytes 1048592 | tf_op jit(solution)/shard_map/all_gather | solution.py:64
  418.5 1.3 copy.30
  419.8 3.9 fusion.2
  423.7 0.1 broadcast_in_dim.58
  423.8 40.5 %psum.7 = f32[128,8]{1,0:T(8,128)S(1)} all-reduce(f32[128,8]{1,0:T(8,128)S(1)} %broadcast_in_dim.58), channel_id=1, replica_groups=mesh['tensor'=4,'example'=8] {'tensor','example'}, use_global_device_ids=true, to_apply=%region_5.6 | all-reduce | flops 1024 | bytes 8192 | tf_op jit(solution)/shard_map/psum | solution.py:72
  464.3 0.1 select_reduce_fusion
  464.5 0.6 bitcast_select_fusion
  (27 shorter events, 0.4 us)
Async XLA Ops:
  6.5 354.6 %copy-start = (s32[8,16]{1,0:T(8,128)S(1)}, s32[8,16]{1,0:T(8,128)}, u32[]{:S(2)}) copy-start(s32[8,16]{1,0:T(8,128)} %param.16) | copy-start | bytes 1540
  6.5 61.4 %all-gather.7.cloned.1.call-start = ((), (), s32[]{:S(2)}) async-start(), calls=%async_computation.2 | async-start | bytes 9437184 | tf_op jit(solution)/shard_map/all_gather | solution.py:43
  7.3 179.7 %reduce-scatter.3.cloned.1.call-start = ((), (), s32[]{:S(2)}) async-start(), calls=%async_computation.3 | async-start | bytes 6553600 | tf_op jit(solution)/shard_map/reduce_scatter | solution.py:47
  77.8 0.9 copy-start.1
  77.8 190.8 %all-gather.9.cloned.1.call-start = ((), (), s32[]{:S(2)}) async-start(), calls=%async_computation.4 | async-start | bytes 5242880 | tf_op jit(solution)/shard_map/all_gather | solution.py:45
  78.6 280.9 %reduce-scatter.5.cloned.1.call-start = ((), (), s32[]{:S(2)}) async-start(), calls=%async_computation.5 | async-start | bytes 11796480 | tf_op jit(solution)/shard_map/reduce_scatter | solution.py:57
  78.9 5.6 %collective-permute-start = (bf16[128,512]{0,1:T(8,128)(2,1)S(1)}, bf16[128,512]{0,1:T(8,128)(2,1)S(1)}, u32[]{:S(2)}, u32[]{:S(2)}) collective-permute-start(bf16[128,512]{0,1:T(8,128)(2,1)S(1)} %copy.23), channel_id=1, source_target_pairs={{0,0},{1,1},{2,8},{3,9},{4,16},{5,17},{6,24},{7,25},{8,2},{9,3},{1... | collective-permute-start | bytes 393224 | tf_op jit(solution)/shard_map/ppermute | solution.py:22
  79.7 4.8 %collective-permute-start.1 = (bf16[128,512]{0,1:T(8,128)(2,1)S(1)}, bf16[128,512]{0,1:T(8,128)(2,1)S(1)}, u32[]{:S(2)}, u32[]{:S(2)}) collective-permute-start(bf16[128,512]{0,1:T(8,128)(2,1)S(1)} %copy.24), channel_id=1, source_target_pairs={{0,1},{1,0},{2,9},{3,8},{4,17},{5,16},{6,25},{7,24},{8,3},{9,2},{1... | collective-permute-start | bytes 393224 | tf_op jit(solution)/shard_map/ppermute | solution.py:22
  279.1 82.0 %copy-start.3 = (s32[128]{0:T(128)S(1)}, s32[128]{0:T(128)}, u32[]{:S(2)}) copy-start(s32[128]{0:T(128)} %param.17) | copy-start | bytes 1540
  279.1 82.0 %copy-start.4 = (s32[128]{0:T(128)S(1)}, s32[128]{0:T(128)}, u32[]{:S(2)}) copy-start(s32[128]{0:T(128)} %param.15) | copy-start | bytes 1540
  279.2 109.9 %all-gather.13.cloned.1.call-start = ((), (), s32[]{:S(2)}) async-start(), calls=%async_computation.7 | async-start | bytes 2359296 | tf_op jit(solution)/shard_map/all_gather | solution.py:54
  280.9 137.5 %all-gather.11.cloned.1.call-start = ((), (), s32[]{:S(2)}) async-start(), calls=%async_computation.6 | async-start | bytes 1310720 | tf_op jit(solution)/shard_map/all_gather | solution.py:64
  396.4 23.4 %copy-start.2 = (bf16[512,1280]{0,1:T(8,128)(2,1)S(1)}, bf16[512,1280]{0,1:T(8,128)(2,1)}, u32[]{:S(2)}) copy-start(bf16[512,1280]{0,1:T(8,128)(2,1)} %reduce-scatter.5.cloned.1.call-done) | copy-start | bytes 3932164
  396.4 23.4 %copy-start.5 = (f32[1024,512]{1,0:T(8,128)S(1)}, f32[1024,512]{1,0:T(8,128)}, u32[]{:S(2)}) copy-start(f32[1024,512]{1,0:T(8,128)} %param.12) | copy-start | bytes 6291460
Sparse Core Ops, SparseCore 0:
  9.2 58.6 all-gather.6
  77.9 108.9 reduce-scatter.2
  188.5 80.0 all-gather.8
  279.3 80.0 reduce-scatter.4
  361.2 27.8 all-gather.12
  390.5 27.9 all-gather.10

commit v2 on v1

--- a/solution.py
+++ b/solution.py
@@ -1,10 +1,346 @@
+import functools
+
 import jax
 import jax.numpy as jnp
 from jax import lax
+from jax.experimental import pallas as pl
+from jax.experimental.pallas import tpu as pltpu
 from jax.sharding import PartitionSpec as P
 
 BF = jnp.bfloat16
 F32 = jnp.float32
+MESH = pl.DeviceIdType.MESH
+VMEM_LIMIT = 56 * 1024 * 1024
+
+
+def flip(index, bit):
+    size = 1 << bit
+    return index + size * (1 - 2 * ((index // size) % 2))
+
+
+def flip_mask(index, mask, bits):
+    for bit in range(bits):
+        if (mask >> bit) & 1:
+            index = flip(index, bit)
+    return index
+
+
+def remote(src, dst, send, recv, **where):
+    return pltpu.make_async_remote_copy(
+        src_ref=src, dst_ref=dst, send_sem=send, recv_sem=recv, device_id=where, device_id_type=MESH
+    )
+
+
+def greet_partners(me, bits):
+    barrier = pltpu.get_barrier_semaphore()
+    for bit in range(bits):
+        pl.semaphore_signal(barrier, inc=1, device_id={"example": flip(me, bit)}, device_id_type=MESH)
+    pl.semaphore_wait(barrier, bits)
+
+
+def level_of(mask, order):
+    for place, bit in enumerate(order):
+        if (mask >> bit) & 1:
+            return place
+    return len(order)
+
+
+def last_level(mask, order):
+    return max(place for place, bit in enumerate(order) if (mask >> bit) & 1)
+
+
+def gather_kernel(bits, x_ref, out_ref, send_sem, recv_sem, local_sem):
+    me = lax.axis_index("example")
+    half = x_ref.shape[0] // 2
+    own = pltpu.make_async_copy(x_ref, out_ref.at[me], local_sem)
+    own.start()
+    greet_partners(me, bits)
+    upper = list(range(1, bits))
+    orders = [upper + [0], upper[::-1] + [0]]
+    started = []
+
+    def view(h, mask):
+        return out_ref.at[flip_mask(me, mask, bits), pl.ds(h * half, half)]
+
+    def send(h, mask, bit):
+        src = x_ref.at[pl.ds(h * half, half)] if mask == 0 else view(h, mask)
+        slot = mask | (1 << bit)
+        copy = remote(src, view(h, mask), send_sem.at[h, slot], recv_sem.at[h, slot], example=flip(me, bit))
+        copy.start()
+        started.append(copy)
+
+    def received(h, mask):
+        remote(view(h, mask), view(h, mask), send_sem.at[h, mask], recv_sem.at[h, mask],
+               example=flip(me, 0)).wait_recv()
+
+    for place in range(bits):
+        for h in range(2):
+            send(h, 0, orders[h][place])
+    arrivals = sorted(
+        ((last_level(mask, orders[h]), bin(mask).count("1"), mask, h) for h in range(2) for mask in range(1, 1 << bits)),
+        key=lambda item: (item[0], item[1], item[3], item[2]),
+    )
+    for place, _, mask, h in arrivals:
+        received(h, mask)
+        for bit in orders[h][place + 1 :]:
+            send(h, mask, bit)
+    for copy in started:
+        copy.wait_send()
+    own.wait()
+
+
+def gather_blocks(x, n_example):
+    bits = n_example.bit_length() - 1
+    return pl.pallas_call(
+        functools.partial(gather_kernel, bits),
+        out_shape=jax.ShapeDtypeStruct((n_example,) + x.shape, x.dtype),
+        in_specs=[pl.BlockSpec(memory_space=pl.ANY)],
+        out_specs=pl.BlockSpec(memory_space=pl.ANY),
+        scratch_shapes=[
+            pltpu.SemaphoreType.DMA((2, n_example)),
+            pltpu.SemaphoreType.DMA((2, n_example)),
+            pltpu.SemaphoreType.DMA,
+        ],
+        compiler_params=pltpu.CompilerParams(collective_id=1, has_side_effects=True),
+        cost_estimate=pl.CostEstimate(flops=0, bytes_accessed=100_000_000, transcendentals=0),
+        name="gather_in_rows",
+    )(x)
+
+
+def line_kernel(n, ratio, left_ref, basis_ref, out_ref, held, inbox, send_sem, recv_sem):
+    t = lax.axis_index("tensor")
+    width = basis_ref.shape[2]
+    barrier = pltpu.get_barrier_semaphore()
+
+    @pl.when(t > 0)
+    def _():
+        pl.semaphore_signal(barrier, inc=1, device_id={"tensor": t - 1}, device_id_type=MESH)
+
+    @pl.when(t < n - 1)
+    def _():
+        pl.semaphore_signal(barrier, inc=1, device_id={"tensor": t + 1}, device_id_type=MESH)
+
+    pl.semaphore_wait(barrier, (t + n - 1) // n + (2 * n - 2 - t) // n)
+
+    def product(block):
+        return jnp.dot(left_ref[...], basis_ref[block], preferred_element_type=F32)
+
+    def copy(way, block, partner):
+        return remote(held.at[block], inbox.at[way, block], send_sem.at[block], recv_sem.at[way, block], tensor=partner)
+
+    late = (2 * t) // n
+
+    def unit(v, carry):
+        u = v // 2
+        way = (v % 2 + late) % 2
+        up = (n - 1 - u // ratio) * ratio + u % ratio
+        block = up + way * (u - up)
+        d = block // ratio
+        sign = 1 - 2 * way
+        place = t + way * (n - 1 - 2 * t)
+        goal = d + way * (n - 1 - 2 * d)
+
+        @pl.when(place < goal)
+        def _():
+            held[block] = product(block).astype(BF)
+
+            @pl.when(place > 0)
+            def _():
+                copy(way, block, t + sign).wait_recv()
+                held[block] = (held[block].astype(F32) + inbox[way, block].astype(F32)).astype(BF)
+
+            copy(way, block, t + sign).start()
+
+        return carry
+
+    lax.fori_loop(0, 2 * n * ratio, unit, 0)
+    for sub in range(ratio):
+        block = t * ratio + sub
+        columns = pl.ds(sub * width, width)
+        held[block] = product(block).astype(BF)
+
+        @pl.when(t > 0)
+        def _():
+            copy(0, block, t - 1).wait_recv()
+            held[block] = (held[block].astype(F32) + inbox[0, block].astype(F32)).astype(BF)
+
+        @pl.when(t < n - 1)
+        def _():
+            copy(1, block, t + 1).wait_recv()
+            held[block] = (held[block].astype(F32) + inbox[1, block].astype(F32)).astype(BF)
+
+        out_ref[:, columns] = held[block]
+
+    def drain(block, carry):
+        d = block // ratio
+
+        @pl.when(d > t)
+        def _():
+            copy(0, block, t + 1).wait_send()
+
+        @pl.when(d < t)
+        def _():
+            copy(1, block, t - 1).wait_send()
+
+        return carry
+
+    lax.fori_loop(0, n * ratio, drain, 0)
+
+
+def line_product(left, blocks, n):
+    count, _, width = blocks.shape
+    rows = left.shape[0]
+    ratio = count // n
+    return pl.pallas_call(
+        functools.partial(line_kernel, n, ratio),
+        out_shape=jax.ShapeDtypeStruct((rows, ratio * width), BF),
+        in_specs=[pl.BlockSpec(memory_space=pltpu.VMEM)] * 2,
+        out_specs=pl.BlockSpec(memory_space=pltpu.VMEM),
+        scratch_shapes=[
+            pltpu.VMEM((count, rows, width), BF),
+            pltpu.VMEM((2, count, rows, width), BF),
+            pltpu.SemaphoreType.DMA((count,)),
+            pltpu.SemaphoreType.DMA((2, count)),
+        ],
+        compiler_params=pltpu.CompilerParams(
+            collective_id=2, has_side_effects=True, vmem_limit_bytes=VMEM_LIMIT
+        ),
+        cost_estimate=pl.CostEstimate(flops=0, bytes_accessed=250_000_000, transcendentals=0),
+        name="line_product",
+    )(left, blocks)
+
+
+def halving_kernel(bits, tile, left_ref, basis_ref, out_ref, held, inbox, send_sem, recv_sem):
+    me = lax.axis_index("example")
+    count = 1 << bits
+    half = left_ref.shape[0] // 2
+    width = held.shape[3]
+    per_block = basis_ref.shape[2] // width
+    greet_partners(me, bits)
+    upper = list(range(1, bits))
+    orders = [[0] + upper, [0] + upper[::-1]]
+
+    def copy(h, mask, place):
+        bit = orders[h][place]
+        kept = mask & ~(1 << bit)
+        where = slots[h][(place, kept)]
+        return remote(held.at[h, mask], inbox.at[h, where], send_sem.at[h, mask], recv_sem.at[h, where],
+                      example=flip(me, bit))
+
+    slots = []
+    for h in range(2):
+        table = {}
+        for place in range(bits):
+            for mask in range(count):
+                if level_of(mask, orders[h]) > place:
+                    table[(place, mask)] = len(table)
+        slots.append(table)
+
+    def priority(mask, order):
+        key = []
+        for place, bit in enumerate(order):
+            key.append(0 if (mask >> bit) & 1 else 1)
+        return key
+
+    started = []
+    units = sorted(
+        ((h, mask) for h in range(2) for mask in range(count)),
+        key=lambda item: (priority(item[1], orders[item[0]]), item[0]),
+    )
+    for h, mask in units:
+        level = level_of(mask, orders[h])
+        for place in range(level):
+            copy(h, mask | (1 << orders[h][place]), place).wait_recv()
+        owner = flip_mask(me, mask, bits)
+        columns = pl.ds(pl.multiple_of((owner % per_block) * width, width), width)
+        inboxes = [slots[h][(place, mask)] for place in range(level)]
+
+        def rows_of(step, carry):
+            rows = pl.ds(pl.multiple_of(step * tile, tile), tile)
+            source = pl.ds(pl.multiple_of(h * half + step * tile, tile), tile)
+            total = jnp.dot(
+                left_ref[source, :], basis_ref[owner // per_block, :, columns], preferred_element_type=F32
+            )
+            total = total.astype(BF).astype(F32)
+            for where in inboxes:
+                total += inbox[h, where, rows, :].astype(F32)
+            if mask == 0:
+                out_ref[source, :] = total.astype(BF)
+            else:
+                held[h, mask, rows, :] = total.astype(BF)
+            return carry
+
+        lax.fori_loop(0, half // tile, rows_of, 0)
+        if mask:
+            sent = copy(h, mask, level)
+            sent.start()
+            started.append(sent)
+    for sent in started:
+        sent.wait_send()
+
+
+def halving_product(left, blocks, n_example):
+    bits = n_example.bit_length() - 1
+    rows = left.shape[0]
+    width = blocks.shape[0] * blocks.shape[2] // n_example
+    half = rows // 2
+    tile = 128
+    while half % tile:
+        tile //= 2
+    return pl.pallas_call(
+        functools.partial(halving_kernel, bits, tile),
+        out_shape=jax.ShapeDtypeStruct((rows, width), BF),
+        in_specs=[pl.BlockSpec(memory_space=pltpu.VMEM)] * 2,
+        out_specs=pl.BlockSpec(memory_space=pltpu.VMEM),
+        scratch_shapes=[
+            pltpu.VMEM((2, n_example, half, width), BF),
+            pltpu.VMEM((2, n_example - 1, half, width), BF),
+            pltpu.SemaphoreType.DMA((2, n_example)),
+            pltpu.SemaphoreType.DMA((2, n_example)),
+        ],
+        compiler_params=pltpu.CompilerParams(
+            collective_id=3, has_side_effects=True, vmem_limit_bytes=VMEM_LIMIT
+        ),
+        cost_estimate=pl.CostEstimate(flops=0, bytes_accessed=150_000_000, transcendentals=0),
+        name="halving_product",
+    )(left, blocks)
+
+
+def total_kernel(steps, x_ref, out_ref, held, inbox, send_sem, recv_sem):
+    barrier = pltpu.get_barrier_semaphore()
+    where = [{axis: flip(lax.axis_index(axis), bit)} for axis, bit in steps]
+    for target in where:
+        pl.semaphore_signal(barrier, inc=1, device_id=target, device_id_type=MESH)
+    pl.semaphore_wait(barrier, len(steps))
+    held[0] = x_ref[...]
+    for k, target in enumerate(where):
+        copy = remote(held.at[k], inbox.at[k], send_sem.at[k], recv_sem.at[k], **target)
+        copy.start()
+        copy.wait()
+        if k + 1 < len(steps):
+            held[k + 1] = held[k] + inbox[k]
+        else:
+            out_ref[...] = held[k] + inbox[k]
+
+
+def total_over_devices(x, n_tensor, n_example):
+    steps = [("example", bit) for bit in range(n_example.bit_length() - 1)]
+    steps += [("tensor", bit) for bit in range(n_tensor.bit_length() - 1)]
+    flat = x.reshape(-1, 128)
+    return pl.pallas_call(
+        functools.partial(total_kernel, steps),
+        out_shape=jax.ShapeDtypeStruct(flat.shape, F32),
+        in_specs=[pl.BlockSpec(memory_space=pltpu.VMEM)],
+        out_specs=pl.BlockSpec(memory_space=pltpu.VMEM),
+        scratch_shapes=[
+            pltpu.VMEM((len(steps),) + flat.shape, F32),
+            pltpu.VMEM((len(steps),) + flat.shape, F32),
+            pltpu.SemaphoreType.DMA((len(steps),)),
+            pltpu.SemaphoreType.DMA((len(steps),)),
+        ],
+        compiler_params=pltpu.CompilerParams(collective_id=4, has_side_effects=True),
+        name="total_scores",
+    )(flat).reshape(x.shape)
 
 
 def regroup_grads(grads, n_tensor, n_example):
@@ -40,36 +376,24 @@
     grads = grad_fac.reshape(-1, width)
     tokens = acts.shape[0]
 
-    in_rows = lax.all_gather(basis_in, "example", axis=1, tiled=True)
     moved_grads = regroup_grads(grads, n_tensor, n_example)
-    out_rows = lax.all_gather(basis_out, "tensor", axis=1, tiled=True)
+    out_rows = lax.all_gather(basis_out, "tensor", axis=0)
+    in_rows = gather_blocks(basis_in, n_example)
     left = jnp.concatenate([queries.reshape(-1, width), acts], axis=0)
-    half_rotated = lax.psum_scatter(
-        jnp.einsum("jl,rj->lr", in_rows, left, preferred_element_type=F32).astype(BF),
-        "tensor",
-        scatter_dimension=0,
-        tiled=True,
-    )
+    half_rotated = line_product(left, in_rows, n_tensor)
     split = query_total * rows
-    acts_rot = lax.all_gather(half_rotated[:, split:], "example", axis=0)
-    parts = [half_rotated[:, q * rows : (q + 1) * rows] for q in range(query_total)]
+    acts_rot = lax.all_gather(half_rotated[split:], "example", axis=0, tiled=True)
+    parts = [half_rotated[q * rows : (q + 1) * rows].T for q in range(query_total)]
     right = jnp.concatenate(parts + [moved_grads], axis=0)
-    core = lax.psum_scatter(
-        jnp.einsum("ik,xi->kx", out_rows, right, preferred_element_type=F32).astype(BF),
-        "example",
-        scatter_dimension=0,
-        tiled=True,
-    )
-    wide = half_rotated.shape[0]
-    grads_rot = lax.all_gather(core[:, query_total * wide :], "tensor", axis=0)
-    acts_flat = jnp.transpose(acts_rot, (1, 0, 2)).reshape(wide, -1).astype(F32)
-    grads_flat = jnp.transpose(grads_rot, (1, 0, 2)).reshape(core.shape[0], -1)
+    core = halving_product(right, out_rows, n_example)
+    wide = half_rotated.shape[1]
+    grads_rot = lax.all_gather(core[query_total * wide :], "tensor", axis=0, tiled=True)
     partial = []
     for q in range(query_total):
-        scaled = (core[:, q * wide : (q + 1) * wide].astype(F32) / eigvals.T).astype(BF)
-        weighted = jnp.einsum("kl,kt->lt", scaled, grads_flat, preferred_element_type=F32)
-        partial.append(jnp.sum(weighted * acts_flat, axis=0))
-    summed = lax.psum(jnp.stack(partial), ("tensor", "example"))
+        scaled = (core[q * wide : (q + 1) * wide].astype(F32) / eigvals).astype(BF)
+        weighted = jnp.einsum("tk,lk->tl", grads_rot, scaled, preferred_element_type=F32)
+        partial.append(jnp.sum(weighted * acts_rot.astype(F32), axis=1))
+    summed = total_over_devices(jnp.stack(partial), n_tensor, n_example)
     by_slot = summed.reshape(query_total, cand_total, token_len)
 
     my_list = lax.dynamic_index_in_dim(score_list, my_index, 0, keepdims=False)

time: 472 us -> 322 us (0.68)
  waiting for transfers between devices: 367 us -> 32.3 us
  Pallas kernels: 0 us -> 258 us
  blocking collectives: 40.5 us -> 0 us
  matrix products: 24.3 us -> 4.21 us
  local copies, waits for them, and re-layouts: 18.4 us -> 5.48 us
    pallas_call x0 -> x4, Pallas kernels: none -> 258 us  [the longest x1 123 us: line_product(): pl.pallas_call(functools.partial(line_kernel, n, ratio), out_shape=jax.Sh...]
    reduce_scatter x2 -> x0, waiting for transfers between devices: 181 us -> none  [the longest x1 102 us: body(): lax.psum_scatter(jnp.einsum('jl,rj->lr', in_rows, left, preferred_element...]
    all_gather x4 -> x3, waiting for transfers between devices: 185 us -> 31.6 us  [the longest x1 31.6 us: body(): lax.all_gather(core[query_total * wide:], 'tensor', axis=0, tiled=True)]
    psum x1 -> x0, blocking collectives: 40.5 us -> none  [body(): summed = lax.psum(jnp.stack(partial), ('tensor', 'example'))]
    dot_general x3 -> x1, matrix products: 24.3 us -> 4.21 us  [body(): jnp.einsum('tk,lk->tl', grads_rot, scaled, preferred_element_type=F32)]
    convert_element_type x1 -> x0, local copies, waits for them, and re-layouts: 5.95 us -> none  [body(): acts_flat = jnp.transpose(acts_rot, (1, 0, 2)).reshape(wide, -1).astype(F32)]
    unnamed x15, local copies, waits for them, and re-layouts: 5.69 us -> 0.57 us
  transfers between devices with their start and end apart: 8 -> 5, of which waited for: 6 -> 1; matrix products, arithmetic and copies ran while one was open for 4% -> 2% of each run, Pallas kernels for 0% -> 75%
where the time goes in v2:
time: 322 us
  Pallas kernels  258 us (80%)
  waiting for transfers between devices  32.3 us (10%)
  between operations  16.9 us (5%)
  local copies, waits for them, and re-layouts  5.48 us (2%)
  matrix products  4.21 us (1%)
  other arithmetic  3.4 us (1%)
    pallas_call x1, Pallas kernels, line_product(): pl.pallas_call(functools.partial(line_kernel, n, ratio), out_shape=jax.Sh...  123 us
    pallas_call x1, Pallas kernels, halving_product(): pl.pallas_call(functools.partial(halving_kernel, bits, tile), out_shape=j...  77.3 us
    pallas_call x1, Pallas kernels, gather_blocks(): pl.pallas_call(functools.partial(gather_kernel, bits), out_shape=jax.Shap...  41.8 us
    all_gather x1, waiting for transfers between devices, body(): lax.all_gather(core[query_total * wide:], 'tensor', axis=0, tiled=True)  31.6 us
    pallas_call x1, Pallas kernels, total_over_devices(): pl.pallas_call(functools.partial(total_kernel, steps), out_shape=jax.Shap...  15.8 us
  transfers between devices with their start and end apart: 5, of which 1 were waited for; matrix products, arithmetic and copies ran while one was open for 2% of the time, Pallas kernels for 75%

profile of v2, /device:TPU:0, one launch (start us, length us, event | category | flops | bytes accessed | tf_op | source)
XLA Modules:
  0.0 321.6 jit_solution(7806934920685727668)
XLA Ops:
  6.5 0.0 copy-start
  6.5 0.7 all-gather.9.cloned.1.call-update
  7.3 0.0 all-gather.7.cloned.1.call-start
  7.3 41.8 %gather_in_rows.1.basis_ref = bf16[8,1024,512]{2,1,0:T(8,128)(2,1)} custom-call(bf16[1024,512]{1,0:T(8,128)(2,1)} %x_ref.1), custom_call_target="tpu_custom_call" | custom-call | bytes 100000000 | tf_op jit(solution)/shard_map/gather_in_rows/pallas_call | solution.py:94
  49.2 1.2 pad_maximum_fusion.left_ref
  50.4 123.4 %line_product.1 = bf16[640,1024]{1,0:T(8,128)(2,1)} custom-call(bf16[640,1024]{1,0:T(8,128)(2,1)} %pad_maximum_fusion.left_ref, bf16[8,1024,512]{2,1,0:T(8,128)(2,1)} %gather_in_rows.1.basis_ref), custom_call_target="tpu_custom_call" | custom-call | bytes 250000000 | tf_op jit(solution)/shard_map/line_product/pallas_call | solution.py:194
  173.8 0.0 slice-start
  173.8 1.8 slice.23
  175.6 0.0 all-gather.7.cloned.1.call-update
  175.6 0.0 all-gather.5.cloned.1.call-start
  175.7 0.7 collective-permute-start
  176.4 0.1 collective-permute-start.1
  176.5 0.6 fusion.7
  179.5 0.5 copy.19
  181.2 0.0 collective-permute-done
  181.2 0.0 collective-permute-done.1
  181.2 0.1 fusion.4
  181.4 1.2 pad_maximum_fusion.1.left_ref
  182.5 77.3 %halving_product.1 = bf16[1280,512]{1,0:T(8,128)(2,1)} custom-call(bf16[1280,512]{1,0:T(8,128)(2,1)} %pad_maximum_fusion.1.left_ref, bf16[4,512,1024]{2,1,0:T(8,128)(2,1)} %bitcast.20), custom_call_target="tpu_custom_call" | custom-call | bytes 150000000 | tf_op jit(solution)/shard_map/halving_product/pallas_call | solution.py:290
  259.9 1.7 slice.21
  261.5 0.0 all-gather.5.cloned.1.call-update
  261.6 0.0 copy-done.4
  261.6 0.0 copy-done.5
  261.6 0.2 select_reduce_fusion.2
  261.8 0.1 iota_compare_fusion
  261.9 31.6 %all-gather.5.cloned.1.call-done = bf16[1024,512]{1,0:T(8,128)(2,1)} async-done(((bf16[256,512]{1,0:T(8,128)(2,1)}), bf16[1024,512]{1,0:T(8,128)(2,1)}) %all-gather.5.cloned.1.call-update) | async-done | bytes 1048592 | tf_op jit(solution)/shard_map/all_gather | solution.py:390
  293.4 4.2 %multiply_reduce_fusion = f32[1024]{0:T(1024)} fusion(bf16[1024,1024]{1,0:T(8,128)(2,1)} %all-gather.7.cloned.1.call-done, bf16[1024,512]{1,0:T(8,128)(2,1)} %all-gather.5.cloned.1.call-done, f32[1024,512]{1,0:T(8,128)S(1)} %copy-done.6, bf16[1280,512]{1,0:T(8,128)(2,1)} %halving_product.1), kind=kOutput, calls=%fused_computation | convolution fusion | flops 1078459392 | bytes 6295552 | tf_op jit(solution)/shard_map/tk,lk->tl/dot_general | solution.py:394
  297.7 15.8 %total_scores.1 = f32[8,128]{1,0:T(8,128)} custom-call(f32[8,128]{1,0:T(8,128)} %bitcast.26), custom_call_target="tpu_custom_call" | custom-call | tf_op jit(solution)/shard_map/total_scores/pallas_call | solution.py:330
  313.5 0.8 broadcast_in_dim.58
  314.3 0.1 select_reduce_fusion
  314.4 0.1 copy.17
  314.5 0.6 bitcast_select_fusion
  (19 shorter events, 0.1 us)
Async XLA Ops:
  6.5 255.0 %copy-start = (s32[8,16]{1,0:T(8,128)S(1)}, s32[8,16]{1,0:T(8,128)}, u32[]{:S(2)}) copy-start(s32[8,16]{1,0:T(8,128)} %param.16) | copy-start | bytes 1540
  6.5 176.0 %all-gather.9.cloned.1.call-start = ((), (), s32[]{:S(2)}) async-start(), calls=%async_computation.2 | async-start | bytes 5242880 | tf_op jit(solution)/shard_map/all_gather | solution.py:380
  7.3 41.9 %copy-start.1 = (bf16[1,512,1024]{2,1,0:T(8,128)(2,1)S(1)}, bf16[1,512,1024]{2,1,0:T(8,128)(2,1)}, u32[]{:S(2)}) copy-start(bf16[1,512,1024]{2,1,0:T(8,128)(2,1)} %param.9) | copy-start | bytes 3145732
  7.3 41.9 %copy-start.2 = (bf16[16,8,1024]{2,1,0:T(8,128)(2,1)S(1)}, bf16[16,8,1024]{2,1,0:T(8,128)(2,1)}, u32[]{:S(2)}) copy-start(bf16[16,8,1024]{2,1,0:T(8,128)(2,1)} %param.13) | copy-start | bytes 786436
  7.3 254.6 %all-gather.7.cloned.1.call-start = ((), (), s32[]{:S(2)}) async-start(), calls=%async_computation.1 | async-start | bytes 2359296 | tf_op jit(solution)/shard_map/all_gather | solution.py:385
  50.3 125.4 %copy-start.3 = (bf16[16,8,1024]{2,1,0:T(8,128)(2,1)S(1)}, bf16[16,8,1024]{2,1,0:T(8,128)(2,1)}, u32[]{:S(2)}) copy-start(bf16[16,8,1024]{2,1,0:T(8,128)(2,1)} %param.14) | copy-start | bytes 786436
  173.8 5.7 %slice-start = ((bf16[640,1024]{1,0:T(8,128)(2,1)}), bf16[512,1024]{1,0:T(8,128)(2,1)S(1)}, s32[]{:S(2)}) async-start(bf16[640,1024]{1,0:T(8,128)(2,1)} %line_product.1), calls=%async_computation.3 | async-start | bytes 2097152 | tf_op jit(solution)/shard_map/slice | solution.py:386
  175.6 117.8 %all-gather.5.cloned.1.call-start = ((), (), s32[]{:S(2)}) async-start(), calls=%async_computation | async-start | bytes 1310720 | tf_op jit(solution)/shard_map/all_gather | solution.py:390
  175.7 5.5 %collective-permute-start = (bf16[128,512]{1,0:T(8,128)(2,1)S(1)}, bf16[128,512]{1,0:T(8,128)(2,1)S(1)}, u32[]{:S(2)}, u32[]{:S(2)}) collective-permute-start(bf16[128,512]{1,0:T(8,128)(2,1)S(1)} %get-tuple-element.10), channel_id=1, source_target_pairs={{0,0},{1,1},{2,8},{3,9},{4,16},{5,17},{6,24},{7,25},{8,2},{9,3},{1... | collective-permute-start | bytes 393224 | tf_op jit(solution)/shard_map/ppermute | solution.py:358
  176.4 4.8 %collective-permute-start.1 = (bf16[128,512]{1,0:T(8,128)(2,1)S(1)}, bf16[128,512]{1,0:T(8,128)(2,1)S(1)}, u32[]{:S(2)}, u32[]{:S(2)}) collective-permute-start(bf16[128,512]{1,0:T(8,128)(2,1)S(1)} %get-tuple-element.9), channel_id=1, source_target_pairs={{0,1},{1,0},{2,9},{3,8},{4,17},{5,16},{6,25},{7,24},{8,3},{9,2},{1... | collective-permute-start | bytes 393224 | tf_op jit(solution)/shard_map/ppermute | solution.py:358
  182.5 79.1 %copy-start.4 = (s32[128]{0:T(128)S(1)}, s32[128]{0:T(128)}, u32[]{:S(2)}) copy-start(s32[128]{0:T(128)} %param.17) | copy-start | bytes 1540
  182.5 79.1 %copy-start.5 = (s32[128]{0:T(128)S(1)}, s32[128]{0:T(128)}, u32[]{:S(2)}) copy-start(s32[128]{0:T(128)} %param.15) | copy-start | bytes 1540
  182.5 110.9 %copy-start.6 = (f32[1024,512]{1,0:T(8,128)S(1)}, f32[1024,512]{1,0:T(8,128)}, u32[]{:S(2)}) copy-start(f32[1024,512]{1,0:T(8,128)} %param.12) | copy-start | bytes 6291460
Sparse Core Ops, SparseCore 0:
  8.9 110.2 all-gather.8
  175.7 36.8 all-gather.6
  261.7 31.7 all-gather.4

commit v3 on v2

--- a/solution.py
+++ b/solution.py
@@ -149,6 +149,12 @@
                 copy(way, block, t + sign).wait_recv()
                 held[block] = (held[block].astype(F32) + inbox[way, block].astype(F32)).astype(BF)
 
+            @pl.when(u >= 2)
+            def _():
+                before = u - 2
+                before_up = (n - 1 - before // ratio) * ratio + before % ratio
+                copy(way, before_up + way * (before - before_up), t + sign).wait_send()
+
             copy(way, block, t + sign).start()
 
         return carry
@@ -171,20 +177,19 @@
 
         out_ref[:, columns] = held[block]
 
-    def drain(block, carry):
-        d = block // ratio
-
-        @pl.when(d > t)
+    def drain(k, carry):
+        @pl.when(t < n - 1)
         def _():
-            copy(0, block, t + 1).wait_send()
-
-        @pl.when(d < t)
+            last = (n - 1 - t) * ratio - 1 - k
+            copy(0, (n - 1 - last // ratio) * ratio + last % ratio, t + 1).wait_send()
+
+        @pl.when(t > 0)
         def _():
-            copy(1, block, t - 1).wait_send()
+            copy(1, t * ratio - 1 - k, t - 1).wait_send()
 
         return carry
 
-    lax.fori_loop(0, n * ratio, drain, 0)
+    lax.fori_loop(0, 2, drain, 0)
 
 
 def line_product(left, blocks, n):
@@ -210,93 +215,149 @@
     )(left, blocks)
 
 
-def halving_kernel(bits, tile, left_ref, basis_ref, out_ref, held, inbox, send_sem, recv_sem):
+def unit_order(bits, orders, parts):
+    masks = range(1 << bits)
+
+    def chunk(pair, keep):
+        found = [(p, mask) for p in pair for mask in masks if keep(mask, orders[p])]
+
+        def key(item):
+            order = orders[item[0]]
+            return ([0 if (item[1] >> bit) & 1 else 1 for bit in order], item[0])
+
+        return sorted(found, key=key)
+
+    def at_level(level):
+        return lambda mask, order: level_of(mask, order) == level
+
+    def first_then(level):
+        return lambda mask, order: level_of(mask, order) == 0 and level_of(mask & ~1, order) == level
+
+    small = [chunk(parts[:2], at_level(level)) for level in range(bits + 1)]
+    large = []
+    for level in range(1, bits + 1):
+        large.append(chunk(parts[2:], first_then(level)))
+        large.append(chunk(parts[2:], at_level(level)))
+    units = []
+    for place in range(max(len(small), len(large))):
+        for chunks in (small, large):
+            if place < len(chunks):
+                units += chunks[place]
+    return units
+
+
+def halving_kernel(bits, n_tensor, core_rows, left_ref, basis_ref, core_ref, grads_ref, held, inbox, send_sem, recv_sem, out_sem, in_sem):
     me = lax.axis_index("example")
+    t = lax.axis_index("tensor")
     count = 1 << bits
-    half = left_ref.shape[0] // 2
-    width = held.shape[3]
+    width = held.shape[2]
     per_block = basis_ref.shape[2] // width
-    greet_partners(me, bits)
+    grad_rows = left_ref.shape[0] - core_rows
+    spans = [
+        (core_rows, grad_rows // 2),
+        (core_rows + grad_rows // 2, grad_rows // 2),
+        (0, core_rows // 2),
+        (core_rows // 2, core_rows // 2),
+    ]
     upper = list(range(1, bits))
-    orders = [[0] + upper, [0] + upper[::-1]]
-
-    def copy(h, mask, place):
-        bit = orders[h][place]
-        kept = mask & ~(1 << bit)
-        where = slots[h][(place, kept)]
-        return remote(held.at[h, mask], inbox.at[h, where], send_sem.at[h, mask], recv_sem.at[h, where],
-                      example=flip(me, bit))
+    orders = [[0] + upper, [0] + upper[::-1]] * 2
+    peers = [(t + k) % n_tensor for k in range(1, n_tensor)]
+    barrier = pltpu.get_barrier_semaphore()
+    for bit in range(bits):
+        pl.semaphore_signal(barrier, inc=1, device_id={"example": flip(me, bit)}, device_id_type=MESH)
+    for peer in peers:
+        pl.semaphore_signal(barrier, inc=1, device_id={"tensor": peer}, device_id_type=MESH)
+    pl.semaphore_wait(barrier, bits + n_tensor - 1)
 
     slots = []
-    for h in range(2):
+    for p in range(4):
         table = {}
         for place in range(bits):
             for mask in range(count):
-                if level_of(mask, orders[h]) > place:
+                if level_of(mask, orders[p]) > place:
                     table[(place, mask)] = len(table)
         slots.append(table)
 
-    def priority(mask, order):
-        key = []
-        for place, bit in enumerate(order):
-            key.append(0 if (mask >> bit) & 1 else 1)
-        return key
+    def copy(p, mask, place):
+        bit = orders[p][place]
+        where = slots[p][(place, mask & ~(1 << bit))]
+        rows = pl.ds(*spans[p])
+        return remote(held.at[mask, rows], inbox.at[where, rows], send_sem.at[p, mask], recv_sem.at[p, where],
+                      example=flip(me, bit))
+
+    def spread(k):
+        rows = grads_ref.at[t]
+        return remote(rows, rows, out_sem.at[k], in_sem.at[k], tensor=peers[k])
 
     started = []
-    units = sorted(
-        ((h, mask) for h in range(2) for mask in range(count)),
-        key=lambda item: (priority(item[1], orders[item[0]]), item[0]),
-    )
-    for h, mask in units:
-        level = level_of(mask, orders[h])
+    finished = 0
+    for p, mask in unit_order(bits, orders, [0, 1, 2, 3]):
+        level = level_of(mask, orders[p])
         for place in range(level):
-            copy(h, mask | (1 << orders[h][place]), place).wait_recv()
+            copy(p, mask | (1 << orders[p][place]), place).wait_recv()
         owner = flip_mask(me, mask, bits)
         columns = pl.ds(pl.multiple_of((owner % per_block) * width, width), width)
-        inboxes = [slots[h][(place, mask)] for place in range(level)]
+        inboxes = [slots[p][(place, mask)] for place in range(level)]
+        start, size = spans[p]
+        tile = 128
+        while size % tile:
+            tile //= 2
 
         def rows_of(step, carry):
-            rows = pl.ds(pl.multiple_of(step * tile, tile), tile)
-            source = pl.ds(pl.multiple_of(h * half + step * tile, tile), tile)
+            rows = pl.ds(pl.multiple_of(start + step * tile, tile), tile)
             total = jnp.dot(
-                left_ref[source, :], basis_ref[owner // per_block, :, columns], preferred_element_type=F32
+                left_ref[rows, :], basis_ref[owner // per_block, :, columns], preferred_element_type=F32
             )
             total = total.astype(BF).astype(F32)
             for where in inboxes:
-                total += inbox[h, where, rows, :].astype(F32)
-            if mask == 0:
-                out_ref[source, :] = total.astype(BF)
+                total += inbox[where, rows, :].astype(F32)
+            if mask:
+                held[mask, rows, :] = total.astype(BF)
+            elif p >= 2:
+                core_ref[rows, :] = total.astype(BF)
             else:
-                held[h, mask, rows, :] = total.astype(BF)
+                grads_ref[t, pl.ds(pl.multiple_of(start - core_rows + step * tile, tile), tile), :] = total.astype(BF)
             return carry
 
-        lax.fori_loop(0, half // tile, rows_of, 0)
+        lax.fori_loop(0, size // tile, rows_of, 0)
         if mask:
-            sent = copy(h, mask, level)
+            sent = copy(p, mask, level)
             sent.start()
             started.append(sent)
+        elif p < 2:
+            finished += 1
+            if finished == 2:
+                for k in range(n_tensor - 1):
+                    spread(k).start()
     for sent in started:
         sent.wait_send()
-
-
-def halving_product(left, blocks, n_example):
+    for k in range(n_tensor - 1):
+        spread(k).wait_send()
+        source = grads_ref.at[(t - 1 - k + n_tensor) % n_tensor]
+        remote(source, source, out_sem.at[k], in_sem.at[k], tensor=peers[k]).wait_recv()
+
+
+def halving_product(left, blocks, n_example, core_rows):
     bits = n_example.bit_length() - 1
     rows = left.shape[0]
-    width = blocks.shape[0] * blocks.shape[2] // n_example
-    half = rows // 2
-    tile = 128
-    while half % tile:
-        tile //= 2
+    n_tensor = blocks.shape[0]
+    width = n_tensor * blocks.shape[2] // n_example
+    vmem = pl.BlockSpec(memory_space=pltpu.VMEM)
     return pl.pallas_call(
-        functools.partial(halving_kernel, bits, tile),
-        out_shape=jax.ShapeDtypeStruct((rows, width), BF),
-        in_specs=[pl.BlockSpec(memory_space=pltpu.VMEM)] * 2,
-        out_specs=pl.BlockSpec(memory_space=pltpu.VMEM),
+        functools.partial(halving_kernel, bits, n_tensor, core_rows),
+        out_shape=(
+            jax.ShapeDtypeStruct((core_rows, width), BF),
+            jax.ShapeDtypeStruct((n_tensor, rows - core_rows, width), BF),
+        ),
+        in_specs=[vmem, vmem],
+        out_specs=(vmem, vmem),
         scratch_shapes=[
-            pltpu.VMEM((2, n_example, half, width), BF),
-            pltpu.VMEM((2, n_example - 1, half, width), BF),
-            pltpu.SemaphoreType.DMA((2, n_example)),
-            pltpu.SemaphoreType.DMA((2, n_example)),
+            pltpu.VMEM((n_example, rows, width), BF),
+            pltpu.VMEM((n_example - 1, rows, width), BF),
+            pltpu.SemaphoreType.DMA((4, n_example)),
+            pltpu.SemaphoreType.DMA((4, n_example)),
+            pltpu.SemaphoreType.DMA((n_tensor - 1,)),
+            pltpu.SemaphoreType.DMA((n_tensor - 1,)),
         ],
         compiler_params=pltpu.CompilerParams(
             collective_id=3, has_side_effects=True, vmem_limit_bytes=VMEM_LIMIT
@@ -385,9 +446,9 @@
     acts_rot = lax.all_gather(half_rotated[split:], "example", axis=0, tiled=True)
     parts = [half_rotated[q * rows : (q + 1) * rows].T for q in range(query_total)]
     right = jnp.concatenate(parts + [moved_grads], axis=0)
-    core = halving_product(right, out_rows, n_example)
     wide = half_rotated.shape[1]
-    grads_rot = lax.all_gather(core[query_total * wide :], "tensor", axis=0, tiled=True)
+    core, grads_rot = halving_product(right, out_rows, n_example, query_total * wide)
+    grads_rot = grads_rot.reshape(-1, core.shape[1])
     partial = []
     for q in range(query_total):
         scaled = (core[q * wide : (q + 1) * wide].astype(F32) / eigvals).astype(BF)

time: 322 us -> 298 us (0.925)
  waiting for transfers between devices: 32.3 us -> 0.75 us
  Pallas kernels: 258 us -> 267 us
    all_gather x1 -> x0, waiting for transfers between devices: 31.6 us -> none  [body(): lax.all_gather(core[query_total * wide:], 'tensor', axis=0, tiled=True)]
    pallas_call x1, Pallas kernels: 77.3 us -> 83.3 us  [halving_product(): pl.pallas_call(functools.partial(halving_kernel, bits, n_tensor, core_row...]
  transfers between devices with their start and end apart: 5 -> 4, of which waited for: 1 -> 0; matrix products, arithmetic and copies ran while one was open for 2% -> 2% of each run, Pallas kernels for 75% -> 84%
where the time goes in v3:
time: 298 us; the launch traced here: 297 us
  Pallas kernels  267 us (90%)
  between operations  17.5 us (6%)
  matrix products  4.21 us (1%)
  local copies, waits for them, and re-layouts  3.87 us (1%)
  other arithmetic  3.41 us (1%)
    pallas_call x1, Pallas kernels, line_product(): pl.pallas_call(functools.partial(line_kernel, n, ratio), out_shape=jax.Sh...  123 us
    pallas_call x1, Pallas kernels, halving_product(): pl.pallas_call(functools.partial(halving_kernel, bits, n_tensor, core_row...  83.3 us
    pallas_call x1, Pallas kernels, gather_blocks(): pl.pallas_call(functools.partial(gather_kernel, bits), out_shape=jax.Shap...  41.8 us
    pallas_call x1, Pallas kernels, total_over_devices(): pl.pallas_call(functools.partial(total_kernel, steps), out_shape=jax.Shap...  18.4 us
  transfers between devices with their start and end apart: 4, of which 0 were waited for; matrix products, arithmetic and copies ran while one was open for 2% of the time, Pallas kernels for 84%

profile of v3, /device:TPU:0, one launch (start us, length us, event | category | flops | bytes accessed | tf_op | source)
XLA Modules:
  0.0 297.5 jit_solution(11269076730555823433)
XLA Ops:
  6.5 0.0 copy-start
  6.5 0.0 all-gather.6.cloned.1.call-start
  6.5 0.7 all-gather.6.cloned.1.call-update
  7.3 0.0 all-gather.4.cloned.1.call-start
  7.3 41.8 %gather_in_rows.1.basis_ref = bf16[8,1024,512]{2,1,0:T(8,128)(2,1)} custom-call(bf16[1024,512]{1,0:T(8,128)(2,1)} %x_ref.1), custom_call_target="tpu_custom_call" | custom-call | bytes 100000000 | tf_op jit(solution)/shard_map/gather_in_rows/pallas_call | solution.py:94
  49.2 1.2 pad_maximum_fusion.left_ref
  50.4 123.4 %line_product.1 = bf16[640,1024]{1,0:T(8,128)(2,1)} custom-call(bf16[640,1024]{1,0:T(8,128)(2,1)} %pad_maximum_fusion.left_ref, bf16[8,1024,512]{2,1,0:T(8,128)(2,1)} %gather_in_rows.1.basis_ref), custom_call_target="tpu_custom_call" | custom-call | bytes 250000000 | tf_op jit(solution)/shard_map/line_product/pallas_call | solution.py:199
  173.8 0.0 slice-start
  173.8 1.8 slice.15
  175.6 0.0 all-gather.4.cloned.1.call-update
  175.7 0.7 collective-permute-start
  176.4 0.1 collective-permute-start.1
  176.5 0.6 fusion.6
  179.6 0.0 copy-start.4
  179.6 0.0 copy-start.5
  179.7 0.5 copy.19
  181.5 0.0 copy-done
  181.5 0.2 select_reduce_fusion.2
  181.7 0.1 iota_compare_fusion
  181.8 0.0 collective-permute-done
  181.8 0.0 collective-permute-done.1
  181.8 0.1 fusion.3
  181.9 1.1 pad_maximum_fusion.1.left_ref
  183.1 83.3 %halving_product.1 = (bf16[1024,512]{1,0:T(8,128)(2,1)}, bf16[4,256,512]{2,1,0:T(8,128)(2,1)}) custom-call(bf16[1280,512]{1,0:T(8,128)(2,1)} %pad_maximum_fusion.1.left_ref, bf16[4,512,1024]{2,1,0:T(8,128)(2,1)} %bitcast.20), custom_call_target="tpu_custom_call" | custom-call | bytes 150000000 | tf_op jit(solution)/shard_map/halving_product/pallas_call | solution.py:346
  266.4 0.0 all-gather.4.cloned.1.call-done
  266.4 0.0 copy-done.6
  266.4 4.2 %multiply_reduce_fusion = f32[1024]{0:T(1024)} fusion(bf16[1024,1024]{1,0:T(8,128)(2,1)} %all-gather.4.cloned.1.call-done, bf16[1024,512]{1,0:T(8,128)(2,1)} %bitcast.28, f32[1024,512]{1,0:T(8,128)S(1)} %copy-done.6, bf16[1024,512]{1,0:T(8,128)(2,1)} %get-tuple-element.8), kind=kOutput, calls=%fused_computation | convolution fusion | flops 1078459392 | bytes 6295552 | tf_op jit(solution)/shard_map/tk,lk->tl/dot_general | solution.py:455
  270.7 18.4 %total_scores.1 = f32[8,128]{1,0:T(8,128)} custom-call(f32[8,128]{1,0:T(8,128)} %bitcast.27), custom_call_target="tpu_custom_call" | custom-call | tf_op jit(solution)/shard_map/total_scores/pallas_call | solution.py:391
  289.0 0.8 broadcast_in_dim.58
  289.8 0.1 select_reduce_fusion
  290.0 0.1 copy.17
  290.0 0.6 bitcast_select_fusion
  (15 shorter events, 0.1 us)
Async XLA Ops:
  6.5 175.0 %copy-start = (s32[8,16]{1,0:T(8,128)S(1)}, s32[8,16]{1,0:T(8,128)}, u32[]{:S(2)}) copy-start(s32[8,16]{1,0:T(8,128)} %param.16) | copy-start | bytes 1540
  6.5 176.5 %all-gather.6.cloned.1.call-start = ((), (), s32[]{:S(2)}) async-start(), calls=%async_computation.1 | async-start | bytes 5242880 | tf_op jit(solution)/shard_map/all_gather | solution.py:441
  7.3 41.9 %copy-start.1 = (bf16[1,512,1024]{2,1,0:T(8,128)(2,1)S(1)}, bf16[1,512,1024]{2,1,0:T(8,128)(2,1)}, u32[]{:S(2)}) copy-start(bf16[1,512,1024]{2,1,0:T(8,128)(2,1)} %param.9) | copy-start | bytes 3145732
  7.3 41.9 %copy-start.2 = (bf16[16,8,1024]{2,1,0:T(8,128)(2,1)S(1)}, bf16[16,8,1024]{2,1,0:T(8,128)(2,1)}, u32[]{:S(2)}) copy-start(bf16[16,8,1024]{2,1,0:T(8,128)(2,1)} %param.13) | copy-start | bytes 786436
  7.3 259.2 %all-gather.4.cloned.1.call-start = ((), (), s32[]{:S(2)}) async-start(), calls=%async_computation | async-start | bytes 2359296 | tf_op jit(solution)/shard_map/all_gather | solution.py:446
  50.4 125.3 %copy-start.3 = (bf16[16,8,1024]{2,1,0:T(8,128)(2,1)S(1)}, bf16[16,8,1024]{2,1,0:T(8,128)(2,1)}, u32[]{:S(2)}) copy-start(bf16[16,8,1024]{2,1,0:T(8,128)(2,1)} %param.14) | copy-start | bytes 786436
  173.8 5.9 %slice-start = ((bf16[640,1024]{1,0:T(8,128)(2,1)}), bf16[512,1024]{1,0:T(8,128)(2,1)S(1)}, s32[]{:S(2)}) async-start(bf16[640,1024]{1,0:T(8,128)(2,1)} %line_product.1), calls=%async_computation.2 | async-start | bytes 2097152 | tf_op jit(solution)/shard_map/slice | solution.py:447
  175.7 6.1 %collective-permute-start = (bf16[128,512]{1,0:T(8,128)(2,1)S(1)}, bf16[128,512]{1,0:T(8,128)(2,1)S(1)}, u32[]{:S(2)}, u32[]{:S(2)}) collective-permute-start(bf16[128,512]{1,0:T(8,128)(2,1)S(1)} %get-tuple-element.14), channel_id=1, source_target_pairs={{0,0},{1,1},{2,8},{3,9},{4,16},{5,17},{6,24},{7,25},{8,2},{9,3},{1... | collective-permute-start | bytes 393224 | tf_op jit(solution)/shard_map/ppermute | solution.py:419
  176.4 5.4 %collective-permute-start.1 = (bf16[128,512]{1,0:T(8,128)(2,1)S(1)}, bf16[128,512]{1,0:T(8,128)(2,1)S(1)}, u32[]{:S(2)}, u32[]{:S(2)}) collective-permute-start(bf16[128,512]{1,0:T(8,128)(2,1)S(1)} %get-tuple-element.13), channel_id=1, source_target_pairs={{0,1},{1,0},{2,9},{3,8},{4,17},{5,16},{6,25},{7,24},{8,3},{9,2},{1... | collective-permute-start | bytes 393224 | tf_op jit(solution)/shard_map/ppermute | solution.py:419
  179.6 1.9 copy-start.4
  179.6 1.9 copy-start.5
  183.1 83.4 %copy-start.6 = (f32[1024,512]{1,0:T(8,128)S(1)}, f32[1024,512]{1,0:T(8,128)}, u32[]{:S(2)}) copy-start(f32[1024,512]{1,0:T(8,128)} %param.12) | copy-start | bytes 6291460
Sparse Core Ops, SparseCore 0:
  8.9 110.2 all-gather.5
  175.7 37.0 all-gather.3

commit v4 on v3

--- a/solution.py
+++ b/solution.py
@@ -49,12 +49,82 @@
     return max(place for place, bit in enumerate(order) if (mask >> bit) & 1)
 
 
-def gather_kernel(bits, x_ref, out_ref, send_sem, recv_sem, local_sem):
+def line_neighbours(t, n):
+    return (t + n - 1) // n + (2 * n - 2 - t) // n
+
+
+def greet_line(barrier, t, n):
+    @pl.when(t > 0)
+    def _():
+        pl.semaphore_signal(barrier, inc=1, device_id={"tensor": t - 1}, device_id_type=MESH)
+
+    @pl.when(t < n - 1)
+    def _():
+        pl.semaphore_signal(barrier, inc=1, device_id={"tensor": t + 1}, device_id_type=MESH)
+
+
+def spread_line(t, n, rows_ref, first, size, parts, send_sem, recv_sem):
+    step = size // parts
+
+    def copy(way, block, part, partner):
+        rows = rows_ref.at[block, pl.ds(first + part * step, step)]
+        return remote(rows, rows, send_sem.at[way, block, part], recv_sem.at[block, part], tensor=partner)
+
+    def begin():
+        for part in range(parts):
+            @pl.when(t < n - 1)
+            def _():
+                copy(0, t, part, t + 1).start()
+
+            @pl.when(t > 0)
+            def _():
+                copy(1, t, part, t - 1).start()
+
+    def relay(far):
+        for part in range(parts):
+            @pl.when(t >= far)
+            def _():
+                copy(0, t - far, part, t - 1).wait_recv()
+
+                @pl.when(t < n - 1)
+                def _():
+                    copy(0, t - far, part, t + 1).start()
+
+            @pl.when(t + far < n)
+            def _():
+                copy(1, t + far, part, t + 1).wait_recv()
+
+                @pl.when(t > 0)
+                def _():
+                    copy(1, t + far, part, t - 1).start()
+
+    def finish():
+        for block in range(n):
+            for part in range(parts):
+                @pl.when((t >= block) & (t < n - 1))
+                def _():
+                    copy(0, block, part, t + 1).wait_send()
+
+                @pl.when((t <= block) & (t > 0))
+                def _():
+                    copy(1, block, part, t - 1).wait_send()
+
+    return begin, relay, finish
+
+
+def gather_kernel(bits, n, early, x_ref, y_ref, out_ref, line_ref, send_sem, recv_sem, local_sem, up_sem, down_sem):
     me = lax.axis_index("example")
     half = x_ref.shape[0] // 2
-    own = pltpu.make_async_copy(x_ref, out_ref.at[me], local_sem)
+    own = pltpu.make_async_copy(x_ref, out_ref.at[me], local_sem.at[0])
     own.start()
-    greet_partners(me, bits)
+    t = lax.axis_index("tensor")
+    mine = pltpu.make_async_copy(y_ref, line_ref.at[t], local_sem.at[1])
+    mine.start()
+    barrier = pltpu.get_barrier_semaphore()
+    for bit in range(bits):
+        pl.semaphore_signal(barrier, inc=1, device_id={"example": flip(me, bit)}, device_id_type=MESH)
+    greet_line(barrier, t, n)
+    pl.semaphore_wait(barrier, bits + line_neighbours(t, n))
     upper = list(range(1, bits))
     orders = [upper + [0], upper[::-1] + [0]]
     started = []
@@ -76,51 +146,64 @@
     for place in range(bits):
         for h in range(2):
             send(h, 0, orders[h][place])
+    mine.wait()
+    begin, relay, finish = spread_line(t, n, line_ref, 0, early, 2, up_sem, down_sem)
+    begin()
     arrivals = sorted(
         ((last_level(mask, orders[h]), bin(mask).count("1"), mask, h) for h in range(2) for mask in range(1, 1 << bits)),
         key=lambda item: (item[0], item[1], item[3], item[2]),
     )
-    for place, _, mask, h in arrivals:
+    turns = [item[0] for item in arrivals]
+    far = 0
+    for turn, (place, _, mask, h) in enumerate(arrivals):
+        if turn and turns[turn - 1] != place and far + 1 < n:
+            far += 1
+            relay(far)
         received(h, mask)
         for bit in orders[h][place + 1 :]:
             send(h, mask, bit)
+    while far + 1 < n:
+        far += 1
+        relay(far)
     for copy in started:
         copy.wait_send()
+    finish()
     own.wait()
 
 
-def gather_blocks(x, n_example):
+def gather_blocks(x, y, n_example, n_tensor, early):
     bits = n_example.bit_length() - 1
+    anywhere = pl.BlockSpec(memory_space=pl.ANY)
     return pl.pallas_call(
-        functools.partial(gather_kernel, bits),
-        out_shape=jax.ShapeDtypeStruct((n_example,) + x.shape, x.dtype),
-        in_specs=[pl.BlockSpec(memory_space=pl.ANY)],
-        out_specs=pl.BlockSpec(memory_space=pl.ANY),
+        functools.partial(gather_kernel, bits, n_tensor, early),
+        out_shape=(
+            jax.ShapeDtypeStruct((n_example,) + x.shape, x.dtype),
+            jax.ShapeDtypeStruct((n_tensor,) + y.shape, y.dtype),
+        ),
+        in_specs=[anywhere] * 2,
+        out_specs=(anywhere,) * 2,
         scratch_shapes=[
             pltpu.SemaphoreType.DMA((2, n_example)),
             pltpu.SemaphoreType.DMA((2, n_example)),
-            pltpu.SemaphoreType.DMA,
+            pltpu.SemaphoreType.DMA((2,)),
+            pltpu.SemaphoreType.DMA((2, n_tensor, 2)),
+            pltpu.SemaphoreType.DMA((n_tensor, 2)),
         ],
         compiler_params=pltpu.CompilerParams(collective_id=1, has_side_effects=True),
         cost_estimate=pl.CostEstimate(flops=0, bytes_accessed=100_000_000, transcendentals=0),
-        name="gather_in_rows",
-    )(x)
-
-
-def line_kernel(n, ratio, left_ref, basis_ref, out_ref, held, inbox, send_sem, recv_sem):
+        name="gather_rows",
+    )(x, y)
+
+
+def line_kernel(n, ratio, early, left_ref, basis_ref, _, out_ref, line_ref, held, inbox, send_sem, recv_sem, up_sem, down_sem):
     t = lax.axis_index("tensor")
     width = basis_ref.shape[2]
     barrier = pltpu.get_barrier_semaphore()
-
-    @pl.when(t > 0)
-    def _():
-        pl.semaphore_signal(barrier, inc=1, device_id={"tensor": t - 1}, device_id_type=MESH)
-
-    @pl.when(t < n - 1)
-    def _():
-        pl.semaphore_signal(barrier, inc=1, device_id={"tensor": t + 1}, device_id_type=MESH)
-
-    pl.semaphore_wait(barrier, (t + n - 1) // n + (2 * n - 2 - t) // n)
+    greet_line(barrier, t, n)
+    pl.semaphore_wait(barrier, line_neighbours(t, n))
+    rest = line_ref.shape[1] - early
+    begin, relay, finish = spread_line(t, n, line_ref, early, rest, 1, up_sem, down_sem)
+    begin()
 
     def product(block):
         return jnp.dot(left_ref[...], basis_ref[block], preferred_element_type=F32)
@@ -132,6 +215,11 @@
 
     def unit(v, carry):
         u = v // 2
+
+        @pl.when((v > 0) & (v % (2 * ratio) == 0))
+        def _():
+            relay(v // (2 * ratio))
+
         way = (v % 2 + late) % 2
         up = (n - 1 - u // ratio) * ratio + u % ratio
         block = up + way * (u - up)
@@ -190,29 +278,38 @@
         return carry
 
     lax.fori_loop(0, 2, drain, 0)
-
-
-def line_product(left, blocks, n):
+    finish()
+
+
+def line_product(left, blocks, out_rows, n, early):
     count, _, width = blocks.shape
     rows = left.shape[0]
     ratio = count // n
+    vmem = pl.BlockSpec(memory_space=pltpu.VMEM)
+    anywhere = pl.BlockSpec(memory_space=pl.ANY)
     return pl.pallas_call(
-        functools.partial(line_kernel, n, ratio),
-        out_shape=jax.ShapeDtypeStruct((rows, ratio * width), BF),
-        in_specs=[pl.BlockSpec(memory_space=pltpu.VMEM)] * 2,
-        out_specs=pl.BlockSpec(memory_space=pltpu.VMEM),
+        functools.partial(line_kernel, n, ratio, early),
+        out_shape=(
+            jax.ShapeDtypeStruct((rows, ratio * width), BF),
+            jax.ShapeDtypeStruct(out_rows.shape, out_rows.dtype),
+        ),
+        in_specs=[vmem, vmem, anywhere],
+        out_specs=(vmem, anywhere),
+        input_output_aliases={2: 1},
         scratch_shapes=[
             pltpu.VMEM((count, rows, width), BF),
             pltpu.VMEM((2, count, rows, width), BF),
             pltpu.SemaphoreType.DMA((count,)),
             pltpu.SemaphoreType.DMA((2, count)),
+            pltpu.SemaphoreType.DMA((2, n, 1)),
+            pltpu.SemaphoreType.DMA((n, 1)),
         ],
         compiler_params=pltpu.CompilerParams(
             collective_id=2, has_side_effects=True, vmem_limit_bytes=VMEM_LIMIT
         ),
         cost_estimate=pl.CostEstimate(flops=0, bytes_accessed=250_000_000, transcendentals=0),
         name="line_product",
-    )(left, blocks)
+    )(left, blocks, out_rows)
 
 
 def unit_order(bits, orders, parts):
@@ -438,10 +535,11 @@
     tokens = acts.shape[0]
 
     moved_grads = regroup_grads(grads, n_tensor, n_example)
-    out_rows = lax.all_gather(basis_out, "tensor", axis=0)
-    in_rows = gather_blocks(basis_in, n_example)
+    early = basis_out.shape[0] * 5 // 8
+    in_rows, out_rows = gather_blocks(basis_in, basis_out, n_example, n_tensor, early)
     left = jnp.concatenate([queries.reshape(-1, width), acts], axis=0)
-    half_rotated = line_product(left, in_rows, n_tensor)
+    left, moved_grads = lax.optimization_barrier((left, moved_grads))
+    half_rotated, out_rows = line_product(left, in_rows, out_rows, n_tensor, early)
     split = query_total * rows
     acts_rot = lax.all_gather(half_rotated[split:], "example", axis=0, tiled=True)
     parts = [half_rotated[q * rows : (q + 1) * rows].T for q in range(query_total)]

time: 298 us -> 349 us (1.17)
  Pallas kernels: 267 us -> 316 us
    pallas_call x2, Pallas kernels: 165 us -> 226 us  [the longest x1 115 us: gather_blocks(): pl.pallas_call(functools.partial(gather_kernel, bits, n_tensor, early), o...]
    pallas_call x1, Pallas kernels: 83.3 us -> 67.6 us  [halving_product(): pl.pallas_call(functools.partial(halving_kernel, bits, n_tensor, core_row...]
    pallas_call x1, Pallas kernels: 18.4 us -> 22.7 us  [total_over_devices(): pl.pallas_call(functools.partial(total_kernel, steps), out_shape=jax.Shap...]
  transfers between devices with their start and end apart: 4 -> 3, of which waited for: 0 -> 0; matrix products, arithmetic and copies ran while one was open for 2% -> 1% of each run, Pallas kernels for 84% -> 52%
where the time goes in v4:
time: 349 us
  Pallas kernels  316 us (91%)
  between operations  17.6 us (5%)
  local copies, waits for them, and re-layouts  6.13 us (2%)
  matrix products  4.26 us (1%)
    pallas_call x1, Pallas kernels, gather_blocks(): pl.pallas_call(functools.partial(gather_kernel, bits, n_tensor, early), o...  115 us
    pallas_call x1, Pallas kernels, line_product(): pl.pallas_call(functools.partial(line_kernel, n, ratio, early), out_shape...  111 us
    pallas_call x1, Pallas kernels, halving_product(): pl.pallas_call(functools.partial(halving_kernel, bits, n_tensor, core_row...  67.6 us
    pallas_call x1, Pallas kernels, total_over_devices(): pl.pallas_call(functools.partial(total_kernel, steps), out_shape=jax.Shap...  22.7 us
  transfers between devices with their start and end apart: 3, of which 0 were waited for; matrix products, arithmetic and copies ran while one was open for 1% of the time, Pallas kernels for 52%

profile of v4, /device:TPU:0, one launch (start us, length us, event | category | flops | bytes accessed | tf_op | source)
XLA Modules:
  0.0 348.9 jit_solution(11276774478212549234)
XLA Ops:
  6.5 0.0 copy-start
  6.5 0.0 all-gather.2.cloned.1.call-start
  6.6 1.1 constant_dynamic-slice_fusion
  7.7 0.7 collective-permute-start
  8.4 0.5 collective-permute-start.1
  8.9 0.7 fusion.6
  13.6 114.8 %gather_rows.1 = (bf16[8,1024,512]{2,1,0:T(8,128)(2,1)}, bf16[4,512,1024]{2,1,0:T(8,128)(2,1)}) custom-call(bf16[1024,512]{1,0:T(8,128)(2,1)} %x_ref.1, bf16[512,1024]{1,0:T(8,128)(2,1)} %y_ref.1), custom_call_target="tpu_custom_call" | custom-call | bytes 100000000 | tf_op jit(solution)/shard_map/gather_rows/pallas_call | solution.py:177
  128.4 0.0 copy-done.1
  128.4 0.0 copy-done.2
  128.4 1.2 pad_maximum_fusion.left_ref
  129.6 0.0 collective-permute-done
  129.6 0.0 collective-permute-done.1
  129.6 0.1 fusion.3
  129.7 0.0 copy-start.3
  129.8 0.0 copy-start.4
  129.8 111.1 %line_product.1 = (bf16[640,1024]{1,0:T(8,128)(2,1)}, bf16[4,512,1024]{2,1,0:T(8,128)(2,1)}) custom-call(bf16[640,1024]{1,0:T(8,128)(2,1)} %pad_maximum_fusion.left_ref, bf16[8,1024,512]{2,1,0:T(8,128)(2,1)} %get-tuple-element.14.basis_ref, bf16[4,512,1024]{2,1,0:T(8,128)(2,1)} %get-tuple-element.15._), custom_call_target="tpu_custom_call", output_to_operand_aliasing={{1}: (2, {})} | custom-call | bytes 250000000 | tf_op jit(solution)/shard_map/line_product/pallas_call | solution.py:290
  240.9 1.7 slice.15
  242.6 0.0 all-gather.2.cloned.1.call-update
  242.6 0.0 copy-done
  242.7 0.2 select_reduce_fusion.2
  242.9 0.1 iota_compare_fusion
  242.9 1.7 copy.15
  244.6 0.1 slice_bitcast_fusion
  244.7 1.1 pad_maximum_fusion.1.left_ref
  245.9 67.6 %halving_product.1 = (bf16[1024,512]{1,0:T(8,128)(2,1)}, bf16[4,256,512]{2,1,0:T(8,128)(2,1)}) custom-call(bf16[1280,512]{1,0:T(8,128)(2,1)} %pad_maximum_fusion.1.left_ref, bf16[4,512,1024]{2,1,0:T(8,128)(2,1)} %get-tuple-element.18.basis_ref), custom_call_target="tpu_custom_call" | custom-call | bytes 150000000 | tf_op jit(solution)/shard_map/halving_product/pallas_call | solution.py:443
  313.5 0.0 all-gather.2.cloned.1.call-done
  313.5 4.3 %multiply_reduce_fusion = f32[1024]{0:T(1024)} fusion(bf16[1024,1024]{1,0:T(8,128)(2,1)} %all-gather.2.cloned.1.call-done, bf16[1024,512]{1,0:T(8,128)(2,1)} %bitcast.26, f32[1024,512]{1,0:T(8,128)S(1)} %copy-done.5, bf16[1024,512]{1,0:T(8,128)(2,1)} %get-tuple-element.20), kind=kOutput, calls=%fused_computation | convolution fusion | flops 1078459392 | bytes 6295552 | tf_op jit(solution)/shard_map/tk,lk->tl/dot_general | solution.py:553
  317.8 22.7 %total_scores.1 = f32[8,128]{1,0:T(8,128)} custom-call(f32[8,128]{1,0:T(8,128)} %bitcast.25), custom_call_target="tpu_custom_call" | custom-call | tf_op jit(solution)/shard_map/total_scores/pallas_call | solution.py:488
  340.5 0.8 broadcast_in_dim.58
  341.3 0.1 select_reduce_fusion
  341.4 0.1 copy.18
  341.5 0.6 bitcast_select_fusion
  (10 shorter events, 0.1 us)
Async XLA Ops:
  6.5 236.1 %copy-start = (s32[8,16]{1,0:T(8,128)S(1)}, s32[8,16]{1,0:T(8,128)}, u32[]{:S(2)}) copy-start(s32[8,16]{1,0:T(8,128)} %param.16) | copy-start | bytes 1540
  6.5 121.9 %copy-start.1 = (bf16[1,512,1024]{2,1,0:T(8,128)(2,1)S(1)}, bf16[1,512,1024]{2,1,0:T(8,128)(2,1)}, u32[]{:S(2)}) copy-start(bf16[1,512,1024]{2,1,0:T(8,128)(2,1)} %param.9) | copy-start | bytes 3145732
  6.5 121.9 %copy-start.2 = (bf16[16,8,1024]{2,1,0:T(8,128)(2,1)S(1)}, bf16[16,8,1024]{2,1,0:T(8,128)(2,1)}, u32[]{:S(2)}) copy-start(bf16[16,8,1024]{2,1,0:T(8,128)(2,1)} %param.13) | copy-start | bytes 786436
  6.5 307.0 %all-gather.2.cloned.1.call-start = ((), (), s32[]{:S(2)}) async-start(), calls=%async_computation | async-start | bytes 2359296 | tf_op jit(solution)/shard_map/all_gather | solution.py:544
  7.7 121.9 %collective-permute-start = (bf16[128,512]{1,0:T(8,128)(2,1)S(1)}, bf16[128,512]{1,0:T(8,128)(2,1)S(1)}, u32[]{:S(2)}, u32[]{:S(2)}) collective-permute-start(bf16[128,512]{1,0:T(8,128)(2,1)S(1)} %get-tuple-element.26), channel_id=1, source_target_pairs={{0,0},{1,1},{2,8},{3,9},{4,16},{5,17},{6,24},{7,25},{8,2},{9,3},{1... | collective-permute-start | bytes 393224 | tf_op jit(solution)/shard_map/ppermute | solution.py:516
  8.4 121.3 %collective-permute-start.1 = (bf16[128,512]{1,0:T(8,128)(2,1)S(1)}, bf16[128,512]{1,0:T(8,128)(2,1)S(1)}, u32[]{:S(2)}, u32[]{:S(2)}) collective-permute-start(bf16[128,512]{1,0:T(8,128)(2,1)S(1)} %get-tuple-element.25), channel_id=1, source_target_pairs={{0,1},{1,0},{2,9},{3,8},{4,17},{5,16},{6,25},{7,24},{8,3},{9,2},{1... | collective-permute-start | bytes 393224 | tf_op jit(solution)/shard_map/ppermute | solution.py:516
  129.7 112.9 %copy-start.3 = (s32[128]{0:T(128)S(1)}, s32[128]{0:T(128)}, u32[]{:S(2)}) copy-start(s32[128]{0:T(128)} %param.17) | copy-start | bytes 1540
  129.8 112.9 %copy-start.4 = (s32[128]{0:T(128)S(1)}, s32[128]{0:T(128)}, u32[]{:S(2)}) copy-start(s32[128]{0:T(128)} %param.15) | copy-start | bytes 1540
  245.9 67.6 %copy-start.5 = (f32[1024,512]{1,0:T(8,128)S(1)}, f32[1024,512]{1,0:T(8,128)}, u32[]{:S(2)}) copy-start(f32[1024,512]{1,0:T(8,128)} %param.12) | copy-start | bytes 6291460
Sparse Core Ops, SparseCore 0:
  242.7 34.3 all-gather.1

commit v5 on v3

--- a/solution.py
+++ b/solution.py
@@ -441,6 +441,7 @@
     out_rows = lax.all_gather(basis_out, "tensor", axis=0)
     in_rows = gather_blocks(basis_in, n_example)
     left = jnp.concatenate([queries.reshape(-1, width), acts], axis=0)
+    left, moved_grads = lax.optimization_barrier((left, moved_grads))
     half_rotated = line_product(left, in_rows, n_tensor)
     split = query_total * rows
     acts_rot = lax.all_gather(half_rotated[split:], "example", axis=0, tiled=True)

time: 298 us -> 283 us (0.950)
  Pallas kernels: 267 us -> 251 us
    pallas_call x1, Pallas kernels: 123 us -> 109 us  [line_product(): pl.pallas_call(functools.partial(line_kernel, n, ratio), out_shape=jax.Sh...]
    pallas_call x1, Pallas kernels: 83.3 us -> 73.3 us  [halving_product(): pl.pallas_call(functools.partial(halving_kernel, bits, n_tensor, core_row...]
    pallas_call x1, Pallas kernels: 41.8 us -> 49.6 us  [gather_blocks(): pl.pallas_call(functools.partial(gather_kernel, bits), out_shape=jax.Shap...]
  transfers between devices with their start and end apart: 4 -> 4, of which waited for: 0 -> 0; matrix products, arithmetic and copies ran while one was open for 2% -> 2% of each run, Pallas kernels for 84% -> 82%
where the time goes in v5:
time: 283 us
  Pallas kernels  251 us (89%)
  between operations  17.5 us (6%)
  local copies, waits for them, and re-layouts  4.81 us (2%)
  matrix products  4.26 us (2%)
  other arithmetic  3.43 us (1%)
    pallas_call x1, Pallas kernels, line_product(): pl.pallas_call(functools.partial(line_kernel, n, ratio), out_shape=jax.Sh...  109 us
    pallas_call x1, Pallas kernels, halving_product(): pl.pallas_call(functools.partial(halving_kernel, bits, n_tensor, core_row...  73.3 us
    pallas_call x1, Pallas kernels, gather_blocks(): pl.pallas_call(functools.partial(gather_kernel, bits), out_shape=jax.Shap...  49.6 us
    pallas_call x1, Pallas kernels, total_over_devices(): pl.pallas_call(functools.partial(total_kernel, steps), out_shape=jax.Shap...  19.4 us
  transfers between devices with their start and end apart: 4, of which 0 were waited for; matrix products, arithmetic and copies ran while one was open for 2% of the time, Pallas kernels for 82%

profile of v5, /device:TPU:0, one launch (start us, length us, event | category | flops | bytes accessed | tf_op | source)
XLA Modules:
  0.0 283.2 jit_solution(4614006667884635556)
XLA Ops:
  6.5 0.7 all-gather.6.cloned.1.call-update
  7.3 0.0 all-gather.4.cloned.1.call-start
  7.3 1.0 constant_dynamic-slice_fusion
  8.3 0.7 collective-permute-start
  9.0 0.5 collective-permute-start.1
  9.5 0.6 fusion.6
  12.7 0.0 copy-start.1
  12.7 0.0 copy-start.2
  12.7 49.6 %gather_in_rows.1.basis_ref = bf16[8,1024,512]{2,1,0:T(8,128)(2,1)} custom-call(bf16[1024,512]{1,0:T(8,128)(2,1)} %x_ref.1), custom_call_target="tpu_custom_call" | custom-call | bytes 100000000 | tf_op jit(solution)/shard_map/gather_in_rows/pallas_call | solution.py:94
  63.6 1.2 pad_maximum_fusion.left_ref
  64.8 0.0 collective-permute-done
  64.8 0.0 collective-permute-done.1
  64.8 0.1 fusion.3
  64.9 0.0 copy-start.3
  64.9 0.0 copy-start.4
  65.0 109.0 %line_product.1 = bf16[640,1024]{1,0:T(8,128)(2,1)} custom-call(bf16[640,1024]{1,0:T(8,128)(2,1)} %pad_maximum_fusion.left_ref, bf16[8,1024,512]{2,1,0:T(8,128)(2,1)} %gather_in_rows.1.basis_ref), custom_call_target="tpu_custom_call" | custom-call | bytes 250000000 | tf_op jit(solution)/shard_map/line_product/pallas_call | solution.py:199
  173.9 0.0 slice-start
  173.9 1.8 slice.15
  175.7 0.0 all-gather.4.cloned.1.call-update
  175.8 0.2 select_reduce_fusion.2
  176.0 0.1 iota_compare_fusion
  176.0 0.5 copy.19
  176.6 1.2 pad_maximum_fusion.1.left_ref
  177.7 73.3 %halving_product.1 = (bf16[1024,512]{1,0:T(8,128)(2,1)}, bf16[4,256,512]{2,1,0:T(8,128)(2,1)}) custom-call(bf16[1280,512]{1,0:T(8,128)(2,1)} %pad_maximum_fusion.1.left_ref, bf16[4,512,1024]{2,1,0:T(8,128)(2,1)} %bitcast.20), custom_call_target="tpu_custom_call" | custom-call | bytes 150000000 | tf_op jit(solution)/shard_map/halving_product/pallas_call | solution.py:346
  251.0 0.0 all-gather.4.cloned.1.call-done
  251.1 0.0 copy-done.5
  251.1 4.3 %multiply_reduce_fusion = f32[1024]{0:T(1024)} fusion(bf16[1024,1024]{1,0:T(8,128)(2,1)} %all-gather.4.cloned.1.call-done, bf16[1024,512]{1,0:T(8,128)(2,1)} %bitcast.28, f32[1024,512]{1,0:T(8,128)S(1)} %copy-done.5, bf16[1024,512]{1,0:T(8,128)(2,1)} %get-tuple-element.12), kind=kOutput, calls=%fused_computation | convolution fusion | flops 1078459392 | bytes 6295552 | tf_op jit(solution)/shard_map/tk,lk->tl/dot_general | solution.py:456
  255.3 19.4 %total_scores.1 = f32[8,128]{1,0:T(8,128)} custom-call(f32[8,128]{1,0:T(8,128)} %bitcast.27), custom_call_target="tpu_custom_call" | custom-call | tf_op jit(solution)/shard_map/total_scores/pallas_call | solution.py:391
  274.7 0.8 broadcast_in_dim.58
  275.5 0.1 select_reduce_fusion
  275.6 0.1 copy.17
  275.7 0.6 bitcast_select_fusion
  (14 shorter events, 0.1 us)
Async XLA Ops:
  6.5 169.2 %copy-start = (s32[8,16]{1,0:T(8,128)S(1)}, s32[8,16]{1,0:T(8,128)}, u32[]{:S(2)}) copy-start(s32[8,16]{1,0:T(8,128)} %param.16) | copy-start | bytes 1540
  6.5 171.2 %all-gather.6.cloned.1.call-start = ((), (), s32[]{:S(2)}) async-start(), calls=%async_computation.1 | async-start | bytes 5242880 | tf_op jit(solution)/shard_map/all_gather | solution.py:441
  7.3 243.8 %all-gather.4.cloned.1.call-start = ((), (), s32[]{:S(2)}) async-start(), calls=%async_computation | async-start | bytes 2359296 | tf_op jit(solution)/shard_map/all_gather | solution.py:447
  8.3 56.4 %collective-permute-start = (bf16[128,512]{1,0:T(8,128)(2,1)S(1)}, bf16[128,512]{1,0:T(8,128)(2,1)S(1)}, u32[]{:S(2)}, u32[]{:S(2)}) collective-permute-start(bf16[128,512]{1,0:T(8,128)(2,1)S(1)} %get-tuple-element.18), channel_id=1, source_target_pairs={{0,0},{1,1},{2,8},{3,9},{4,16},{5,17},{6,24},{7,25},{8,2},{9,3},{1... | collective-permute-start | bytes 393224 | tf_op jit(solution)/shard_map/ppermute | solution.py:419
  9.0 55.8 %collective-permute-start.1 = (bf16[128,512]{1,0:T(8,128)(2,1)S(1)}, bf16[128,512]{1,0:T(8,128)(2,1)S(1)}, u32[]{:S(2)}, u32[]{:S(2)}) collective-permute-start(bf16[128,512]{1,0:T(8,128)(2,1)S(1)} %get-tuple-element.17), channel_id=1, source_target_pairs={{0,1},{1,0},{2,9},{3,8},{4,17},{5,16},{6,25},{7,24},{8,3},{9,2},{1... | collective-permute-start | bytes 393224 | tf_op jit(solution)/shard_map/ppermute | solution.py:419
  12.7 50.9 %copy-start.1 = (bf16[1,512,1024]{2,1,0:T(8,128)(2,1)S(1)}, bf16[1,512,1024]{2,1,0:T(8,128)(2,1)}, u32[]{:S(2)}) copy-start(bf16[1,512,1024]{2,1,0:T(8,128)(2,1)} %param.9) | copy-start | bytes 3145732
  12.7 50.9 %copy-start.2 = (bf16[16,8,1024]{2,1,0:T(8,128)(2,1)S(1)}, bf16[16,8,1024]{2,1,0:T(8,128)(2,1)}, u32[]{:S(2)}) copy-start(bf16[16,8,1024]{2,1,0:T(8,128)(2,1)} %param.13) | copy-start | bytes 786436
  64.9 110.8 %copy-start.3 = (s32[128]{0:T(128)S(1)}, s32[128]{0:T(128)}, u32[]{:S(2)}) copy-start(s32[128]{0:T(128)} %param.17) | copy-start | bytes 1540
  64.9 110.8 %copy-start.4 = (s32[128]{0:T(128)S(1)}, s32[128]{0:T(128)}, u32[]{:S(2)}) copy-start(s32[128]{0:T(128)} %param.15) | copy-start | bytes 1540
  173.9 2.1 slice-start
  177.7 73.3 %copy-start.5 = (f32[1024,512]{1,0:T(8,128)S(1)}, f32[1024,512]{1,0:T(8,128)}, u32[]{:S(2)}) copy-start(f32[1024,512]{1,0:T(8,128)} %param.12) | copy-start | bytes 6291460
Sparse Core Ops, SparseCore 0:
  8.9 95.0 all-gather.5
  175.8 36.0 all-gather.3
